TPU v7x, 32 devices: a whole 2x2x4 slice. The times are simulated.
32 devices in a mesh: kv: 2 (over y), ctx: 16 (over z, x, core).
Axes of the slice: x: 2, y: 2, z: 4, core: 2. Of those that a mesh axis runs over, the one named last changes fastest.
Arguments:
- residual: bfloat16 [64, 8192], P(None, 'ctx'), may hold values from -8 to 8
- queries: bfloat16 [64, 8192], P(None, 'kv'), may hold values from -16 to 16
- draft_token_keys: bfloat16 [64, 1024], P(None, 'kv'), may hold values from -32 to 32
- draft_token_values: bfloat16 [64, 1024], P(None, 'kv'), may hold values from -8 to 8
- cache_keys: bfloat16 [2, 8192, 1024], P(None, 'ctx', 'kv'), may hold values from -32 to 32
- cached_value_rows: bfloat16 [2, 8192, 1024], P(None, 'ctx', 'kv'), may hold values from -8 to 8
- tenant_ids: int32 [64], replicated, may hold values from 0 to 1, as said below
- tree_mask: int32 [64, 64], replicated, may hold values from 0 to 1, as said below
- cache_lengths: int32 [2], replicated, may hold values from 4097 to 8192
- out_weight: bfloat16 [8192, 8192], P('kv', 'ctx'), may hold values from -0.0625 to 0.0625
- out_signs: bfloat16 [2, 8192, 8192], P(None, 'kv', 'ctx'), may hold values from -1 to 1, as said below
- norm_gain: float32 [8192], P('ctx'), may hold values from 0.1 to 1.9
- gate_weight: bfloat16 [8192, 16384], P(None, ('kv', 'ctx')), may hold values from -0.0625 to 0.0625
- up_weight: bfloat16 [8192, 16384], P(None, ('kv', 'ctx')), may hold values from -0.0625 to 0.0625
- down_weight: bfloat16 [16384, 8192], P(('kv', 'ctx')), may hold values from -0.09375 to 0.09375
- gate_signs: bfloat16 [2, 8192, 16384], P(None, None, ('kv', 'ctx')), may hold values from -1 to 1, as said below
- up_signs: bfloat16 [2, 8192, 16384], P(None, None, ('kv', 'ctx')), may hold values from -1 to 1, as said below
- down_signs: bfloat16 [2, 16384, 8192], P(None, ('kv', 'ctx')), may hold values from -1 to 1, as said below
- delta_scale: float32 [2, 4], replicated, may hold values from 0.3 to 0.9
Outputs:
- mixed: bfloat16 [64, 8192], P(None, 'ctx')
Inputs may be any that keep to these rules, and one draw needn't show every extreme that they name: `tenant_ids`: exactly 32 tokens belong to each tenant. `tree_mask`: entry (i, j) is 1 exactly when token j is token i or an ancestor of token i in the draft tree of their common tenant; each tenant's 32 tokens form one tree. `out_signs`: every entry is 1 or -1. `gate_signs`: every entry is 1 or -1. `up_signs`: every entry is 1 or -1. `down_signs`: every entry is 1 or -1.
All inputs are finite; a program needn't handle non-finite values.
Results may differ from a plain program's by a relative error of at most 0.013.
Values may be sent and summed in bfloat16 or wider, within the bound.
No kernel may reach another device: no remote copies, remote signals or barrier semaphores. Data moves between devices by JAX's collectives and lax.ppermute only.
A program may use at most 192 MiB of HBM per device.

v0:
```python
import functools

import jax
import jax.numpy as jnp
from jax import lax
from jax.experimental import pallas as pl
from jax.experimental.pallas import tpu as pltpu
from jax.sharding import PartitionSpec as P

HEAD_SIZE = 128
LANES = 128
STAT_ROWS = 16
NEG = -1e30
EPS = 1e-05
LOG2E = 1.4426950408889634
SLOTS = 4
MIB = 1 << 20
F32 = jnp.float32
BF16 = jnp.bfloat16


IN_VMEM = pl.BlockSpec(memory_space=pltpu.VMEM)
IN_SMEM = pl.BlockSpec(memory_space=pltpu.SMEM)
IN_HBM = pl.BlockSpec(memory_space=pl.ANY)


def vmem(x):
    return pltpu.with_memory_space_constraint(x, pltpu.VMEM)


def hbm(x):
    return pltpu.with_memory_space_constraint(x, pltpu.HBM)


def call(kernel, scalars, arrays, shapes, far=(), scratch=(), limit=4 * MIB, far_out=False):
    if far_out:
        out_shape = [jax.ShapeDtypeStruct(s, d) for s, d in shapes]
    else:
        out_shape = [pltpu.VMEM(s, d) for s, d in shapes]
    return pl.pallas_call(
        kernel,
        in_specs=[IN_SMEM] * len(scalars) + [IN_VMEM] * len(arrays) + [IN_HBM] * len(far),
        out_specs=[IN_VMEM] * len(shapes),
        out_shape=out_shape,
        scratch_shapes=list(scratch),
        compiler_params=pltpu.CompilerParams(vmem_limit_bytes=limit),
    )(*scalars, *[vmem(a) for a in arrays], *[hbm(a) for a in far])


def iota(shape, dim):
    return lax.broadcasted_iota(jnp.int32, shape, dim)


def to_row(column):
    rows = column.shape[0]
    diagonal = iota((rows, LANES), 0) == iota((rows, LANES), 1)
    return jnp.sum(jnp.where(diagonal, column, 0.0), axis=0, keepdims=True)


def to_column(row, rows):
    diagonal = iota((rows, LANES), 0) == iota((rows, LANES), 1)
    return jnp.sum(jnp.where(diagonal, row, 0.0), axis=1, keepdims=True)


def pack_row(row):
    high = row.astype(BF16).astype(F32)
    middle = (row - high).astype(BF16).astype(F32)
    low = row - high - middle
    place = iota((STAT_ROWS, LANES), 0)
    packed = jnp.where(place == 0, high, jnp.where(place == 1, middle, low))
    return jnp.where(place < 3, packed, 0.0).astype(BF16)


def unpack_row(block):
    return jnp.sum(block.astype(F32), axis=0, keepdims=True)


def reversed_bits(value, bits):
    out = 0
    for i in range(bits):
        out = out | (((value >> i) & 1) << (bits - 1 - i))
    return out


def start_halves(copies, rows):
    def half(h, carry):
        for copy in copies(pl.multiple_of(h * (rows // 2), rows // 2), rows // 2):
            copy.start()
        return carry

    lax.fori_loop(0, 2, half, 0)


def attention_kernel(bits, n_raw, me_ref, len_ref, *refs):
    ids_hbm, tree_hbm, q_hbm, dk_hbm, dv_hbm, k_hbm, v_hbm, res_hbm, gain_hbm, w_hbm, s_hbm = refs[:11]
    keep_ref, send_ref, pm_ref, res_ref, gain_ref = refs[11:16]
    raw_refs = refs[16 : 16 + n_raw]
    ids_ref, tree_ref, q_ref, dk_ref, dv_ref, k_ref, v_ref, sems, raw_sems = refs[16 + n_raw :]
    tenants, slots, _ = k_ref.shape
    small = [
        pltpu.make_async_copy(source, target, sems.at[i])
        for i, (source, target) in enumerate(
            [
                (ids_hbm, ids_ref), (tree_hbm, tree_ref), (q_hbm, q_ref), (dk_hbm, dk_ref),
                (dv_hbm, dv_ref), (res_hbm, res_ref), (gain_hbm, gain_ref),
            ]
        )
    ]
    cache = []
    for t in range(tenants):
        at = len(small) + 2 * t
        cache.append(
            [
                pltpu.make_async_copy(k_hbm.at[t], k_ref.at[t], sems.at[at]),
                pltpu.make_async_copy(v_hbm.at[t], v_ref.at[t], sems.at[at + 1]),
            ]
        )

    def raw_copies(first, rows):
        for i, out in enumerate(raw_refs):
            at, to = pl.ds(i * out.shape[2] + first, rows), pl.ds(first, rows)
            yield pltpu.make_async_copy(w_hbm.at[at], out.at[0, 0, to], raw_sems.at[i, 0])
            for t in range(tenants):
                yield pltpu.make_async_copy(
                    s_hbm.at[t, at], out.at[0, 1 + t, to], raw_sems.at[i, 1 + t]
                )

    for copy in small + [c for pair in cache for c in pair]:
        copy.start()

    tokens = tree_ref.shape[0]
    draft = tokens // tenants
    groups = dk_ref.shape[1] // HEAD_SIZE
    width = q_ref.shape[1] // dk_ref.shape[1]
    me = me_ref[0]
    core = me & 1
    rows = keep_ref.shape[1] - STAT_ROWS
    parts = width * draft // rows
    factor = HEAD_SIZE ** (-0.5)
    power = factor * LOG2E
    nt = (((1,), (1,)), ((), ()))

    for copy in small:
        copy.wait()
    a = iota((tokens, tokens), 0)
    b = iota((tokens, tokens), 1)
    across = jnp.broadcast_to(ids_ref[...], (tokens, tokens))
    along = jnp.sum(jnp.where(a == b, across, 0), axis=1, keepdims=True)
    before = (along < across) | ((along == across) & (a < b))
    place = jnp.sum(before.astype(jnp.int32), axis=0, keepdims=True)
    choose = (place == a).astype(F32).astype(BF16)
    pm_ref[...] = choose
    seen_all = jnp.dot(choose, tree_ref[...].astype(F32).astype(BF16), preferred_element_type=F32)
    seen_all = jnp.where(me == 0, seen_all, 0.0)
    mine = jnp.dot(choose, q_ref[...], preferred_element_type=F32).astype(BF16)

    for t in range(tenants):
        seen = jnp.concatenate([seen_all[t * draft : (t + 1) * draft]] * width, axis=0) > 0.5
        live = me * slots + iota((1, slots), 1) < len_ref[t]
        for copy in cache[t]:
            copy.wait()
        if t == 0:
            start_halves(raw_copies, raw_refs[0].shape[2])
        for g in range(groups):
            head = slice(g * HEAD_SIZE, (g + 1) * HEAD_SIZE)
            query = jnp.concatenate(
                [
                    mine[
                        t * draft : (t + 1) * draft,
                        (g * width + w) * HEAD_SIZE : (g * width + w + 1) * HEAD_SIZE,
                    ]
                    for w in range(width)
                ],
                axis=0,
            )
            far = lax.dot_general(query, k_ref[t, :, head], nt, preferred_element_type=F32)
            near = lax.dot_general(query, dk_ref[:, head], nt, preferred_element_type=F32)
            far = jnp.where(live, far, NEG)
            near = jnp.where(seen, near, NEG)
            peak = jnp.maximum(
                jnp.max(far, axis=1, keepdims=True), jnp.max(near, axis=1, keepdims=True)
            )
            some = peak > 0.5 * NEG
            far = jnp.exp2((far - peak) * power)
            near = jnp.exp2((near - peak) * power)
            total = jnp.sum(far, axis=1, keepdims=True) + jnp.sum(near, axis=1, keepdims=True)
            value = jnp.dot(far.astype(BF16), v_ref[t, :, head], preferred_element_type=F32)
            value = value + jnp.dot(near.astype(BF16), dv_ref[:, head], preferred_element_type=F32)
            value = value * (1.0 / total)
            level = jnp.where(some, peak * factor + jnp.log(total), NEG)
            for i in range(0, parts, 2):
                even = value[i * rows : (i + 1) * rows]
                odd = value[(i + 1) * rows : (i + 2) * rows]
                even_level = to_row(level[i * rows : (i + 1) * rows])
                odd_level = to_row(level[(i + 1) * rows : (i + 2) * rows])
                block = (t * groups + g) * parts + i
                where = reversed_bits((block >> 1) ^ (me >> 1), bits - 1)
                first = core == 0
                keep_ref[where, :rows, :] = jnp.where(first, even, odd).astype(BF16)
                send_ref[where, :rows, :] = jnp.where(first, odd, even).astype(BF16)
                keep_ref[where, rows:, :] = pack_row(jnp.where(first, even_level, odd_level))
                send_ref[where, rows:, :] = pack_row(jnp.where(first, odd_level, even_level))
    for copy in raw_copies(0, raw_refs[0].shape[2]):
        copy.wait()


def attention_partials(
    me, lengths, tenant_ids, tree, queries, dk, dv, keys, values, residual, gain, weight, signs, n
):
    tenants = keys.shape[0]
    tokens = tenant_ids.shape[0]
    groups = dk.shape[1] // HEAD_SIZE
    width = queries.shape[1] // dk.shape[1]
    rows = tokens * groups * width // n
    depth, features = weight.shape
    deep = min(512, depth)
    n_raw = depth // deep
    part = ((n // 2, rows + STAT_ROWS, HEAD_SIZE), BF16)
    gain = gain.reshape(1, features)
    ids = tenant_ids.reshape(1, tokens)
    inner = [ids, tree, queries, dk, dv, keys, values]
    return call(
        functools.partial(attention_kernel, n.bit_length() - 1, n_raw),
        [me, lengths],
        [],
        [part, part, ((tokens, tokens), BF16), (residual.shape, BF16), (gain.shape, F32)]
        + [((1, 1 + tenants, deep, features), BF16)] * n_raw,
        far=inner + [residual, gain, weight, signs],
        scratch=[pltpu.VMEM(x.shape, x.dtype) for x in inner]
        + [
            pltpu.SemaphoreType.DMA((7 + 2 * tenants,)),
            pltpu.SemaphoreType.DMA((n_raw, 1 + tenants)),
        ],
        limit=12 * MIB,
    )


def merged(a_ref, i, b_ref, j, rows):
    a = unpack_row(a_ref[i, rows:, :])
    b = unpack_row(b_ref[j, rows:, :])
    peak = jnp.maximum(a, b)
    ea = jnp.exp(a - peak)
    eb = jnp.exp(b - peak)
    total = ea + eb
    wa = to_column(ea / total, rows)
    mine = a_ref[i, :rows, :].astype(F32)
    value = b_ref[j, :rows, :].astype(F32)
    return (value + (mine - value) * wa).astype(BF16), peak + jnp.log(total)


def merge_kernel(keep_ref, got_ref, token_ref, *outs):
    count = got_ref.shape[0]
    rows = keep_ref.shape[1] - STAT_ROWS
    for i in range(count):
        value, level = merged(keep_ref, i, got_ref, i, rows)
        per_out = count // len(outs)
        out, j = outs[i // per_out], i % per_out
        out[j, :rows, :] = value
        out[j, rows:, :] = pack_row(level)


def merge(keep, got, token):
    count, tall, lanes = got.shape
    outs = 1 if count == 2 else 2
    shapes = [((count // outs, tall, lanes), BF16)] * outs
    return call(merge_kernel, [], [keep, got, token], shapes)


def finish_rows_kernel(own_ref, got_ref, token_ref, o_ref):
    rows = o_ref.shape[1]
    for i in range(2):
        o_ref[i] = merged(own_ref, i, got_ref, 1 - i, rows)[0]


def finish_rows(own, got, token):
    _, tall, lanes = own.shape
    return call(
        finish_rows_kernel, [], [own, got, token],
        [((2, tall - STAT_ROWS, lanes), BF16)],
    )[0]


def join_kernel(a_ref, b_ref, token_ref, o_ref):
    count = a_ref.shape[0]
    o_ref[:count] = a_ref[...]
    o_ref[count:] = b_ref[...]


def join(a, b, token):
    shape = (a.shape[0] + b.shape[0],) + a.shape[1:]
    return call(join_kernel, [], [a, b, token], [(shape, a.dtype)])[0]


class Load:
    def __init__(self, source, kind, scale, pieces, first, ordered, by_column, shape):
        self.source, self.kind, self.scale = source, kind, scale
        self.pieces, self.first = pieces, first
        self.ordered, self.by_column, self.shape = ordered, by_column, shape

    def views(self, me, bits, w, s, first=0, count=None):
        rows, columns = self.shape
        count = count or rows
        for g in range(self.pieces):
            block = self.first + g
            if self.ordered:
                block = reversed_bits(block, bits) ^ me
            if self.by_column:
                at = (
                    pl.ds(first, count),
                    pl.ds(pl.multiple_of(block * columns, columns), columns),
                )
            else:
                at = (pl.ds(pl.multiple_of(block * rows, rows) + first, count),)
            yield w.at[at], [s.at[(t,) + at] for t in range(s.shape[0])]


def load_kernel(bits, loads, n_sources, n_tokens, tenants, me_ref, scale_ref, *refs):
    me = me_ref[0]
    refs = refs[n_tokens:]
    sources, refs = refs[: 2 * n_sources], refs[2 * n_sources :]
    outs, token_ref, refs = refs[: len(loads)], refs[len(loads)], refs[len(loads) + 1 :]
    token_ref[...] = jnp.zeros_like(token_ref)
    kinds = list(dict.fromkeys((l.pieces,) + l.shape for l in loads))
    buffers = {kind: (refs[2 * i], refs[2 * i + 1]) for i, kind in enumerate(kinds)}
    queue, seen = [], {kind: 0 for kind in kinds}
    for load, out in zip(loads, outs):
        kind = (load.pieces,) + load.shape
        buffer, sems = buffers[kind]
        slot = seen[kind] % SLOTS
        seen[kind] += 1
        copies = []
        w, s = sources[2 * load.source], sources[2 * load.source + 1]
        for g, (base, signs) in enumerate(load.views(me, bits, w, s)):
            for i, view in enumerate([base] + signs):
                copies.append(
                    pltpu.make_async_copy(
                        view, buffer.at[slot, i, g], sems.at[slot, g * (tenants + 1) + i]
                    )
                )
        queue.append((load, out, buffer, slot, copies))
    ahead = SLOTS
    for item in queue[:ahead]:
        for copy in item[-1]:
            copy.start()
    for i, (load, out, buffer, slot, copies) in enumerate(queue):
        for copy in copies:
            copy.wait()
        rows = load.shape[0]
        step = min(64, rows)
        scales = [scale_ref[t, load.kind] * load.scale for t in range(tenants)]

        def combine(k, carry, out=out, buffer=buffer, slot=slot, scales=scales, load=load):
            at = pl.ds(pl.multiple_of(k * step, step), step)
            for g in range(load.pieces):
                base = buffer[slot, 0, g, at, :].astype(F32)
                for t in range(tenants):
                    sign = buffer[slot, 1 + t, g, at, :].astype(F32)
                    out[g, t, at, :] = (base + scales[t] * sign).astype(BF16)
            return carry

        lax.fori_loop(0, rows // step, combine, 0)
        if i + ahead < len(queue):
            for copy in queue[i + ahead][-1]:
                copy.start()


def load(me, scale, bits, loads, sources, tokens, tenants):
    used = sorted({l.source for l in loads})
    loads = [
        Load(
            used.index(l.source), l.kind, l.scale, l.pieces, l.first, l.ordered, l.by_column, l.shape
        )
        for l in loads
    ]
    far = [x for i in used for x in sources[i]]
    kinds = list(dict.fromkeys((l.pieces,) + l.shape for l in loads))
    scratch = []
    for pieces, rows, columns in kinds:
        scratch.append(pltpu.VMEM((SLOTS, tenants + 1, pieces, rows, columns), BF16))
        scratch.append(pltpu.SemaphoreType.DMA((SLOTS, pieces * (tenants + 1))))
    shapes = [((l.pieces, tenants) + l.shape, BF16) for l in loads] + [((8, LANES), F32)]
    *blocks, token = call(
        functools.partial(load_kernel, bits, loads, len(used), len(tokens), tenants),
        [me, scale],
        tokens,
        shapes,
        far=far,
        scratch=scratch,
        limit=(7 * len(kinds)) * MIB,
    )
    return blocks, token


def weighted(x, block, piece, scales):
    tenants = len(scales)
    draft = x.shape[0] // tenants
    raw = block.shape[1] > tenants
    parts = [
        jnp.dot(
            x[t * draft : (t + 1) * draft], block[piece, raw + t], preferred_element_type=F32
        )
        for t in range(tenants)
    ]
    if not raw:
        return jnp.concatenate(parts, axis=0)
    base = jnp.dot(x, block[piece, 0], preferred_element_type=F32)
    return base + jnp.concatenate([scales[t] * parts[t] for t in range(tenants)], axis=0)


def out_kernel(bits, factor, me_ref, scale_ref, low_ref, high_ref, *rest):
    *w_refs, o_ref, all_ref, x_ref = rest
    half, rows, _ = low_ref.shape
    n = 2 * half
    tenants = w_refs[0].shape[1] - 1
    draft = x_ref.shape[0] // tenants
    me = me_ref[0]
    all_ref[:half] = low_ref[...]
    all_ref[half:] = high_ref[...]
    heads = rows // draft
    for block in range(n):
        where = reversed_bits(block ^ me, bits)
        t, inside = divmod(block, n // tenants)
        for h in range(heads):
            column = (inside * heads + h) * HEAD_SIZE
            x_ref[t * draft : (t + 1) * draft, column : column + HEAD_SIZE] = all_ref[
                where, h * draft : (h + 1) * draft, :
            ]
    base, delta, at = 0.0, [0.0] * tenants, 0
    for w in w_refs:
        deep = w.shape[2]
        x = x_ref[:, at : at + deep]
        base = base + jnp.dot(x, w[0, 0], preferred_element_type=F32)
        for t in range(tenants):
            delta[t] = delta[t] + jnp.dot(
                x[t * draft : (t + 1) * draft], w[0, 1 + t], preferred_element_type=F32
            )
        at += deep
    for t in range(tenants):
        own = slice(t * draft, (t + 1) * draft)
        o_ref[own, :] = (base[own] + scale_ref[t, 0] * factor * delta[t]).astype(BF16)


def out_projection(me, scale, factor, low, high, weights, tokens):
    half, rows, lanes = low.shape
    features = weights[0].shape[-1]
    depth = sum(w.shape[2] for w in weights)
    return call(
        functools.partial(out_kernel, (2 * half).bit_length() - 1, factor),
        [me, scale],
        [low, high] + weights,
        [((tokens, features), BF16)],
        scratch=[pltpu.VMEM((2 * half, rows, lanes), BF16), pltpu.VMEM((tokens, depth), BF16)],
    )[0]


def hidden_kernel(pm_ref, residual_ref, gain_ref, own_ref, got_ref, token_ref, hidden_ref, send_ref):
    tokens = own_ref.shape[0]
    hidden = jnp.dot(pm_ref[...], residual_ref[...], preferred_element_type=F32) + (
        own_ref[...].astype(F32) + got_ref[...].astype(F32)
    )
    hidden_ref[...] = hidden
    scaled = (hidden * gain_ref[...]).astype(BF16)
    pieces = hidden.shape[1] // LANES
    for f in range(pieces):
        send_ref[0, f * tokens : (f + 1) * tokens, :] = scaled[:, f * LANES : (f + 1) * LANES]
    squares = jnp.sum(hidden * hidden, axis=1, keepdims=True)
    send_ref[0, pieces * tokens :, :] = pack_row(to_row(squares))


def hidden_block(pm, residual, gain, own, got, token):
    tokens, features = own.shape
    tall = features // LANES * tokens + STAT_ROWS
    return call(
        hidden_kernel,
        [],
        [pm, residual, gain, own, got, token],
        [((tokens, features), F32), ((1, tall, LANES), BF16)],
    )


def gate_up_kernel(first, last, bits, counts, n_jobs, loads, width, me_ref, *rest):
    n_x = len(counts)
    x_refs, rest = rest[:n_x], rest[n_x + 1 :]
    g_refs, u_refs, rest = rest[:n_jobs], rest[n_jobs : 2 * n_jobs], rest[2 * n_jobs :]
    before = ()
    if not first:
        before, rest = rest[:3], rest[3:]
    if loads:
        w_hbm, s_hbm, *rest = rest
        *rest, sems = rest
        split = 1 if last else 3
        rest, raw_refs = rest[:split], rest[split:]

        def raw_copies(first, rows):
            for i, (load, out) in enumerate(zip(loads, raw_refs)):
                k = 0
                views = load.views(me_ref[0], bits, w_hbm, s_hbm, first, rows)
                for g, (base, signs) in enumerate(views):
                    for j, view in enumerate([base] + signs):
                        to = out.at[g, j, pl.ds(first, rows)]
                        yield pltpu.make_async_copy(view, to, sems.at[i, k])
                        k += 1

        start_halves(raw_copies, loads[0].shape[0])
    tokens = rest[0].shape[0]
    pieces, tenants = g_refs[0].shape[:2]
    draft = tokens // tenants
    columns = (x_refs[0].shape[1] - STAT_ROWS) // tokens
    squares = jnp.zeros((STAT_ROWS, LANES), F32) if first else before[2][...]
    for x_ref, count in zip(x_refs, counts):
        for i in range(count):
            squares = squares + x_ref[i, columns * tokens :, :].astype(F32)
    if last:
        norm = to_column(
            lax.rsqrt(jnp.sum(squares, axis=0, keepdims=True) / width + EPS), tokens
        )
    else:
        rest[2][...] = squares
    for t in range(tenants):
        own = slice(t * draft, (t + 1) * draft)
        sums = [0.0, 0.0] if first else [before[j][own, :] for j in range(2)]
        block = 0
        for x_ref, count in zip(x_refs, counts):
            for i in range(count):
                x = jnp.concatenate(
                    [
                        x_ref[i, f * tokens + t * draft : f * tokens + (t + 1) * draft, :]
                        for f in range(columns)
                    ],
                    axis=1,
                )
                job, piece = divmod(block, pieces)
                block += 1
                for j, refs in enumerate((g_refs, u_refs)):
                    sums[j] = sums[j] + jnp.dot(
                        x, refs[job][piece, t], preferred_element_type=F32
                    )
        if last:
            gate = sums[0] * norm[own]
            up = sums[1] * norm[own]
            rest[0][own, :] = (gate / (1.0 + jnp.exp(-gate)) * up).astype(BF16)
        else:
            rest[0][own, :] = sums[0]
            rest[1][own, :] = sums[1]
    if loads:
        for copy in raw_copies(0, loads[0].shape[0]):
            copy.wait()


def gate_up(me, bits, xs, token, gates, ups, tokens, width, before=(), last=False, loads=(), source=()):
    units = gates[0].shape[-1]
    if last:
        shapes = [((tokens, units), BF16)]
    else:
        shapes = [((tokens, units), F32)] * 2 + [((STAT_ROWS, LANES), F32)]
    scratch = []
    if loads:
        tenants = source[1].shape[0]
        shapes += [((l.pieces, 1 + tenants) + l.shape, BF16) for l in loads]
        scratch = [pltpu.SemaphoreType.DMA((len(loads), loads[0].pieces * (1 + tenants)))]
    counts = tuple(x.shape[0] for x in xs)
    out = call(
        functools.partial(
            gate_up_kernel, not before, last, bits, counts, len(gates), loads, width
        ),
        [me],
        list(xs) + [token] + gates + ups + list(before),
        shapes,
        far=source if loads else (),
        scratch=scratch,
    )
    split = 1 if last else 3
    return out[:split], out[split:]


def down_kernel(factor, n_outs, scale_ref, x_ref, token_ref, *rest):
    w_refs, o_refs = rest[:-n_outs], rest[-n_outs:]
    pieces = w_refs[0].shape[0]
    tenants = scale_ref.shape[0]
    scales = [scale_ref[t, 3] * factor for t in range(tenants)]
    x = x_ref[...]
    per_out = o_refs[0].shape[0]
    for i in range(per_out * n_outs):
        job, piece = divmod(i, pieces)
        total = weighted(x, w_refs[job], piece, scales)
        o_refs[i // per_out][i % per_out] = total.astype(BF16)


def down(scale, factor, active, token, weights, outs):
    features = weights[0].shape[-1]
    tokens = active.shape[0]
    shape = (weights[0].shape[0] * len(weights) // outs, tokens, features)
    return call(
        functools.partial(down_kernel, factor, outs), [scale],
        [active, token] + weights, [(shape, BF16)] * outs,
    )


def add_kernel(keep_ref, got_ref, *outs):
    count = got_ref.shape[0]
    per_out = count // len(outs)
    for i in range(count):
        total = (keep_ref[i].astype(F32) + got_ref[i].astype(F32)).astype(BF16)
        outs[i // per_out][i % per_out] = total


def add(keep, got, outs):
    count, tokens, features = got.shape
    return call(add_kernel, [], [keep, got], [((count // outs, tokens, features), BF16)] * outs)


def finish_kernel(pm_ref, hidden_ref, own_ref, got_ref, o_ref):
    mixed = hidden_ref[...] + (own_ref[0].astype(F32) + got_ref[0].astype(F32))
    o_ref[...] = lax.dot_general(
        pm_ref[...], mixed.astype(BF16), (((0,), (0,)), ((), ())), preferred_element_type=F32
    ).astype(BF16)


def finish(pm, hidden, own, got):
    return call(finish_kernel, [], [pm, hidden, own, got], [(hidden.shape, BF16)], far_out=True)[0]


def layer(
    residual,
    queries,
    draft_token_keys,
    draft_token_values,
    cache_keys,
    cached_value_rows,
    tenant_ids,
    tree_mask,
    cache_lengths,
    out_weight,
    out_signs,
    norm_gain,
    gate_weight,
    up_weight,
    down_weight,
    gate_signs,
    up_signs,
    down_signs,
    delta_scale,
):
    n = lax.axis_size("ctx")
    bits = n.bit_length() - 1
    me = lax.axis_index("ctx").astype(jnp.int32).reshape(1)
    tokens = tenant_ids.shape[0]
    tenants = cache_keys.shape[0]
    features = residual.shape[1]
    all_features, units = gate_weight.shape
    n_kv = lax.axis_size("kv")
    out_factor = (out_weight.shape[0] * n_kv) ** (-0.5)
    unit_factor = all_features ** (-0.5)
    down_factor = (units * n * n_kv) ** (-0.5)
    scale = delta_scale

    def swap(x, bit):
        return lax.ppermute(x, "ctx", [(i, i ^ (1 << bit)) for i in range(n)])

    def swap_kv(x):
        return lax.ppermute(x, "kv", [(i, (i + 1) % n_kv) for i in range(n_kv)])

    sources = [(gate_weight, gate_signs), (up_weight, up_signs), (down_weight, down_signs)]
    pieces = max(1, n // 16)
    eighth, quarter, half = n // 8, n // 4, n // 2
    todo = []
    spans = [(0, 3 * eighth), (half, 7 * eighth), (3 * eighth, half), (7 * eighth, n)]
    for i in [i for a, b in spans for i in range(a, b, pieces)]:
        shape = (features, units)
        todo.append((("gate", i), Load(0, 1, unit_factor, pieces, i, True, False, shape)))
        todo.append((("up", i), Load(1, 2, unit_factor, pieces, i, True, False, shape)))
    downs = [
        (("down", i), Load(2, 3, down_factor, pieces, i, True, True, (units, features)))
        for i in list(range(half, n, pieces)) + list(range(0, half, pieces))
    ]
    n_raw = min(RAW_DOWN, len(downs))
    todo += downs[: len(downs) - n_raw]
    late = downs[len(downs) - n_raw :]
    held = {}

    def fill(count, *tokens_in):
        nonlocal todo
        now, todo = todo[:count], todo[count:]
        if not now:
            return tokens_in[0]
        blocks, token = load(
            me, scale, bits, [l for _, l in now], sources, list(tokens_in), tenants
        )
        for (name, _), block in zip(now, blocks):
            held[name] = block
        return token

    keep, send, pm, residual_here, gain, *out_raw = attention_partials(
        me, cache_lengths, tenant_ids, tree_mask, queries, draft_token_keys, draft_token_values,
        cache_keys, cached_value_rows, residual, norm_gain, out_weight, out_signs, n,
    )
    plan = (PLAN_DOWN + [0] * bits)[: bits - 1]
    for bit in range(bits - 1):
        got = swap(send, bit)
        token = fill(plan[bit], send)
        out = merge(keep, got, token)
        if bit < bits - 2:
            keep, send = out
    (both,) = out
    got = swap(both, bits - 1)
    token = fill(PLAN_TURN, both)
    rows = finish_rows(both, got, token)
    plan = ([0] * bits + PLAN_UP)[-(bits - 2) :]
    for i, bit in enumerate(reversed(range(1, bits - 1))):
        got = swap(rows, bit)
        token = fill(plan[i], rows)
        rows = join(rows, got, token)
    other = swap(rows, 0)
    own = out_projection(me, scale, out_factor, rows, other, out_raw, tokens)

    got = swap_kv(own)
    token = fill(PLAN_LAST[0], own)
    hidden, block = hidden_block(pm, residual_here, gain, own, got, token)
    for bit in reversed(range(3, bits)):
        got = swap(block, bit)
        token = fill(PLAN_LAST[1], block)
        block = join(block, got, token)

    def gate_up_of(xs, spans, token, **options):
        names = [i for a, b in spans for i in range(a, b, pieces)]
        return gate_up(
            me, bits, xs, token, [held["gate", i] for i in names], [held["up", i] for i in names],
            tokens, all_features, **options,
        )

    got_z = swap(block, 2)
    got_x = swap(block, 1)
    got_core = swap(block, 0)
    token = fill(len(todo), block)
    sums, _ = gate_up_of([block], [(0, eighth)], token)
    far_x = swap(got_z, 1)
    got_core_2 = swap(join(got_z, got_x, sums[2]), 0)
    sums, raw = gate_up_of(
        [got_z, got_x, got_core, got_core_2],
        [(eighth, 3 * eighth), (half, 7 * eighth)],
        sums[2],
        before=sums,
        loads=tuple(l for _, l in late),
        source=sources[2],
    )
    for (name, _), array in zip(late, raw):
        held[name] = array
    got_core_3 = swap(far_x, 0)
    sums, _ = gate_up_of([far_x], [(3 * eighth, half)], sums[2], before=sums)
    (active,), _ = gate_up_of(
        [got_core_3], [(7 * eighth, n)], sums[2], before=sums, last=True
    )

    def down_of(a, b, token, outs):
        weights = [held["down", i] for i in range(a, b, pieces)]
        return down(scale, down_factor, active, token, weights, outs)

    send_near, send_far = down_of(half, n, active, 2)
    got_far = swap(send_far, 0)
    got_near = swap(send_near, 0)
    (mine_far,) = down_of(quarter, half, send_near, 1)
    x_late, x_early = add(mine_far, got_far, 2)
    got_early = swap(x_early, 1)
    got_late = swap(x_late, 1)
    (mine_near,) = down_of(0, quarter, x_early, 1)
    keep, send = add(mine_near, got_near, 2)
    (send,) = add(send, got_early, 1)
    got = swap(send, 2)
    (keep,) = add(keep, got_late, 1)
    for bit in range(3, bits):
        keep, send = add(keep, got, 2)
        got = swap(send, bit)
    (total,) = add(keep, got, 1)
    return finish(pm, hidden, total, swap_kv(total))


PLAN_DOWN = [2, 5, 3]
PLAN_TURN = 5
PLAN_UP = [3, 6]
PLAN_LAST = [5, 5]
RAW_DOWN = 8


def solution(mesh):
    return jax.shard_map(
        layer,
        mesh=mesh,
        in_specs=(
            P(None, "ctx"),
            P(None, "kv"),
            P(None, "kv"),
            P(None, "kv"),
            P(None, "ctx", "kv"),
            P(None, "ctx", "kv"),
            P(),
            P(),
            P(),
            P("kv", "ctx"),
            P(None, "kv", "ctx"),
            P("ctx"),
            P(None, ("kv", "ctx")),
            P(None, ("kv", "ctx")),
            P(("kv", "ctx"), None),
            P(None, None, ("kv", "ctx")),
            P(None, None, ("kv", "ctx")),
            P(None, ("kv", "ctx"), None),
            P(),
        ),
        out_specs=P(None, "ctx"),
        check_vma=False,
    )
```

profile of v0, /device:TPU:0, one launch (start us, length us, event | category | flops | bytes accessed | tf_op | source)
XLA Modules:
  0.0 105.2 jit_solution(4351775933439957309)
XLA Ops:
  0.0 0.7 copy-done.1
  0.7 6.9 %shard_map.181 = (bf16[8,144,128]{2,1,0:T(8,128)(2,1)S(1)}, bf16[8,144,128]{2,1,0:T(8,128)(2,1)S(1)}, bf16[64,64]{1,0:T(8,128)(2,1)S(1)}, bf16[64,512]{1,0:T(8,1...) custom-call(s32[1]{0:T(128)} %bitcast.me_ref, ...), custom_call_target="tpu_custom_call" | custom-call | tf_op jit(solution)/shard_map/pallas_call | solution.py:40
  7.6 0.6 collective-permute-start
  8.1 2.8 %shard_map.182 = (bf16[1,2,512,512]{3,2,1,0:T(8,128)(2,1)S(1)}, bf16[1,2,512,512]{3,2,1,0:T(8,128)(2,1)S(1)}, f32[8,128]{1,0:T(8,128)S(1)}) custom-call(s32[1]{0:T(128)} %bitcast.me_ref, f32[2,4]{1,0:T(2,128)S(1)} %copy-done, bf16[8,144,128]{2,1,0:T(8,128)(2,1)S(1)} %get-tuple-element.102.refs_0_, bf16[8192,512]{1,0:T(8,128)(2,1)} %refs_1_.18, ...), custom_call_target="tpu_custom_call" | custom-call | tf_op jit(solution)/shard_map/pallas_call | solution.py:40
  10.9 0.0 collective-permute-done.got_ref
  11.0 0.2 shard_map.183
  11.2 2.6 %collective-permute-start.1 = (bf16[4,144,128]{2,1,0:T(8,128)(2,1)S(1)}, bf16[4,144,128]{2,1,0:T(8,128)(2,1)S(1)}, u32[]{:S(2)}, u32[]{:S(2)}) collective-permute-start(bf16[4,144,128]{2,1,0:T(8,128)(2,1)S(1)} %get-tuple-element.105.refs_0_), channel_id=1, source_target_pairs={{0,2},{1,3},{2,0},{3,1},{4,6},{5,7},{6,4},{7,5},{8,10},{9,11},{10,... | collective-permute-start | bytes 442376 | tf_op jit(solution)/shard_map/ppermute | solution.py:658
  13.8 4.4 %shard_map.184 = (bf16[1,2,512,512]{3,2,1,0:T(8,128)(2,1)S(1)}, bf16[1,2,512,512]{3,2,1,0:T(8,128)(2,1)S(1)}, bf16[1,2,512,512]{3,2,1,0:T(8,128)(2,1)S(1)}, bf16...) custom-call(s32[1]{0:T(128)} %bitcast.me_ref, f32[2,4]{1,0:T(2,128)S(1)} %copy-done, ...), custom_call_target="tpu_custom_call" | custom-call | tf_op jit(solution)/shard_map/pallas_call | solution.py:40
  18.2 0.1 collective-permute-done.1.got_ref
  18.3 0.2 shard_map.185
  18.4 1.9 %collective-permute-start.2 = (bf16[2,144,128]{2,1,0:T(8,128)(2,1)S(1)}, bf16[2,144,128]{2,1,0:T(8,128)(2,1)S(1)}, u32[]{:S(2)}, u32[]{:S(2)}) collective-permute-start(bf16[2,144,128]{2,1,0:T(8,128)(2,1)S(1)} %get-tuple-element.108.refs_0_), channel_id=1, source_target_pairs={{0,4},{1,5},{2,6},{3,7},{4,0},{5,1},{6,2},{7,3},{8,12},{9,13},{10,... | collective-permute-start | bytes 221192 | tf_op jit(solution)/shard_map/ppermute | solution.py:658
  20.3 3.3 %shard_map.186 = (bf16[1,2,512,512]{3,2,1,0:T(8,128)(2,1)S(1)}, bf16[1,2,512,512]{3,2,1,0:T(8,128)(2,1)S(1)}, bf16[1,2,512,512]{3,2,1,0:T(8,128)(2,1)S(1)}, f32[8,128]{1,0:T(8,128)S(1)}) custom-call(s32[1]{0:T(128)} %bitcast.me_ref, f32[2,4]{1,0:T(2,128)S(1)} %copy-done, bf16[2,144,128]{2,1,0:T(8,128)(2,1)S(1)} %get-tuple-element.108.refs_0_, ...), custom_call_target="tpu_custom_call" | custom-call | tf_op jit(solution)/shard_map/pallas_call | solution.py:40
  23.6 0.0 collective-permute-done.2.got_ref
  23.6 0.1 shard_map.187.refs_0_.own_ref
  23.7 2.7 %collective-permute-start.3 = (bf16[2,144,128]{2,1,0:T(8,128)(2,1)S(1)}, bf16[2,144,128]{2,1,0:T(8,128)(2,1)S(1)}, u32[]{:S(2)}, u32[]{:S(2)}) collective-permute-start(bf16[2,144,128]{2,1,0:T(8,128)(2,1)S(1)} %shard_map.187.refs_0_.own_ref), channel_id=1, source_target_pairs={{0,8},{1,9},{2,10},{3,11},{4,12},{5,13},{6,14},{7,15},{8,0},{9,1},... | collective-permute-start | bytes 221192 | tf_op jit(solution)/shard_map/ppermute | solution.py:658
  26.4 4.4 %shard_map.188 = (bf16[1,2,512,512]{3,2,1,0:T(8,128)(2,1)S(1)}, bf16[1,2,512,512]{3,2,1,0:T(8,128)(2,1)S(1)}, bf16[1,2,512,512]{3,2,1,0:T(8,128)(2,1)S(1)}, bf16...) custom-call(s32[1]{0:T(128)} %bitcast.me_ref, f32[2,4]{1,0:T(2,128)S(1)} %copy-done, ...), custom_call_target="tpu_custom_call" | custom-call | tf_op jit(solution)/shard_map/pallas_call | solution.py:40
  30.8 0.1 shard_map.189.refs_0_.a_ref
  31.0 1.1 %collective-permute-start.4 = (bf16[2,128,128]{2,1,0:T(8,128)(2,1)S(1)}, bf16[2,128,128]{2,1,0:T(8,128)(2,1)S(1)}, u32[]{:S(2)}, u32[]{:S(2)}) collective-permute-start(bf16[2,128,128]{2,1,0:T(8,128)(2,1)S(1)} %shard_map.189.refs_0_.a_ref), channel_id=1, source_target_pairs={{0,4},{1,5},{2,6},{3,7},{4,0},{5,1},{6,2},{7,3},{8,12},{9,13},{10,... | collective-permute-start | bytes 196616 | tf_op jit(solution)/shard_map/ppermute | solution.py:658
  32.1 3.3 %shard_map.190 = (bf16[1,2,512,512]{3,2,1,0:T(8,128)(2,1)S(1)}, bf16[1,2,512,512]{3,2,1,0:T(8,128)(2,1)S(1)}, bf16[1,2,512,512]{3,2,1,0:T(8,128)(2,1)S(1)}, f32[8,128]{1,0:T(8,128)S(1)}) custom-call(s32[1]{0:T(128)} %bitcast.me_ref, f32[2,4]{1,0:T(2,128)S(1)} %copy-done, bf16[2,128,128]{2,1,0:T(8,128)(2,1)S(1)} %shard_map.189.refs_0_.a_ref, ...), custom_call_target="tpu_custom_call" | custom-call | tf_op jit(solution)/shard_map/pallas_call | solution.py:40
  35.4 0.0 collective-permute-done.4.b_ref
  35.4 1.6 %collective-permute-start.5 = (bf16[4,128,128]{2,1,0:T(8,128)(2,1)S(1)}, bf16[4,128,128]{2,1,0:T(8,128)(2,1)S(1)}, u32[]{:S(2)}, u32[]{:S(2)}) collective-permute-start(bf16[4,128,128]{2,1,0:T(8,128)(2,1)S(1)} %shard_map.191.refs_0_.a_ref), channel_id=1, source_target_pairs={{0,2},{1,3},{2,0},{3,1},{4,6},{5,7},{6,4},{7,5},{8,10},{9,11},{10,... | collective-permute-start | bytes 393224 | tf_op jit(solution)/shard_map/ppermute | solution.py:658
  37.0 4.8 %shard_map.192 = (bf16[1,2,512,512]{3,2,1,0:T(8,128)(2,1)S(1)}, bf16[1,2,512,512]{3,2,1,0:T(8,128)(2,1)S(1)}, bf16[1,2,512,512]{3,2,1,0:T(8,128)(2,1)S(1)}, bf16...) custom-call(s32[1]{0:T(128)} %bitcast.me_ref, ...), custom_call_target="tpu_custom_call" | custom-call | tf_op jit(solution)/shard_map/pallas_call | solution.py:40
  41.8 0.1 collective-permute-start.6
  41.9 1.5 %collective-permute-done.6.high_ref = bf16[8,128,128]{2,1,0:T(8,128)(2,1)S(1)} collective-permute-done((bf16[8,128,128]{2,1,0:T(8,128)(2,1)S(1)}, bf16[8,128,128]{2,1,0:T(8,128)(2,1)S(1)}, u32[]{:S(2)}, u32[]{:S(2)}) %collective-permute-start.6) | collective-permute-done | bytes 262176 | tf_op jit(solution)/shard_map/ppermute | solution.py:658
  43.4 2.8 %shard_map.194.refs_0_.own_ref = bf16[64,512]{1,0:T(8,128)(2,1)S(1)} custom-call(s32[1]{0:T(128)} %bitcast.me_ref, f32[2,4]{1,0:T(2,128)S(1)} %copy-done, bf16[8,128,128]{2,1,0:T(8,128)(2,1)S(1)} %shard_map.193.low_ref, bf16[8,128,128]{2,1,0:T(8,128)(2,1)S(1)} %collective-permute-done.6.high_ref, bf16[1,3,512,512]{3,2,1,0:T(8,128)(2,1)S(1)} %get-tuple-element.113.rest_0_, ...), custom_call_target="tpu_custom_call" | custom-call | tf_op jit(solution)/shard_map/pallas_call | solution.py:40
  46.3 1.6 %collective-permute-start.7 = (bf16[64,512]{1,0:T(8,128)(2,1)S(1)}, bf16[64,512]{1,0:T(8,128)(2,1)S(1)}, u32[]{:S(2)}, u32[]{:S(2)}) collective-permute-start(bf16[64,512]{1,0:T(8,128)(2,1)S(1)} %shard_map.194.refs_0_.own_ref), channel_id=1, source_target_pairs={{0,16},{16,0},{1,17},{17,1},{2,18},{18,2},{3,19},{19,3},{4,20},{20... | collective-permute-start | bytes 196616 | tf_op jit(solution)/shard_map/ppermute | solution.py:661
  47.8 4.4 %shard_map.195 = (bf16[1,2,512,512]{3,2,1,0:T(8,128)(2,1)S(1)}, bf16[1,2,512,512]{3,2,1,0:T(8,128)(2,1)S(1)}, bf16[1,2,512,512]{3,2,1,0:T(8,128)(2,1)S(1)}, bf16...) custom-call(s32[1]{0:T(128)} %bitcast.me_ref, f32[2,4]{1,0:T(2,128)S(1)} %copy-done, ...), custom_call_target="tpu_custom_call" | custom-call | tf_op jit(solution)/shard_map/pallas_call | solution.py:40
  52.3 0.2 shard_map.196
  52.5 1.7 %collective-permute-start.8 = (bf16[1,272,128]{2,1,0:T(8,128)(2,1)S(1)}, bf16[1,272,128]{2,1,0:T(8,128)(2,1)S(1)}, u32[]{:S(2)}, u32[]{:S(2)}) collective-permute-start(bf16[1,272,128]{2,1,0:T(8,128)(2,1)S(1)} %get-tuple-element.123.refs_0_.a_ref), channel_id=1, source_target_pairs={{0,8},{1,9},{2,10},{3,11},{4,12},{5,13},{6,14},{7,15},{8,0},{9,1},... | collective-permute-start | bytes 208904 | tf_op jit(solution)/shard_map/ppermute | solution.py:658
  54.2 4.4 %shard_map.197 = (bf16[1,2,512,512]{3,2,1,0:T(8,128)(2,1)S(1)}, bf16[1,2,512,512]{3,2,1,0:T(8,128)(2,1)S(1)}, bf16[1,2,512,512]{3,2,1,0:T(8,128)(2,1)S(1)}, bf16...) custom-call(s32[1]{0:T(128)} %bitcast.me_ref, f32[2,4]{1,0:T(2,128)S(1)} %copy-done, ...), custom_call_target="tpu_custom_call" | custom-call | tf_op jit(solution)/shard_map/pallas_call | solution.py:40
  58.6 0.3 collective-permute-done.8.b_ref
  58.9 0.6 collective-permute-start.12
  59.5 0.7 collective-permute-start.9
  60.2 4.9 %shard_map.199 = (bf16[1,2,512,512]{3,2,1,0:T(8,128)(2,1)S(1)}, bf16[1,2,512,512]{3,2,1,0:T(8,128)(2,1)S(1)}, bf16[1,2,512,512]{3,2,1,0:T(8,128)(2,1)S(1)}, bf16...) custom-call(s32[1]{0:T(128)} %bitcast.me_ref, ...), custom_call_target="tpu_custom_call" | custom-call | tf_op jit(solution)/shard_map/pallas_call | solution.py:40
  65.1 0.8 shard_map.200
  66.0 0.0 collective-permute-done.12.b_ref.rest_1_
  66.0 0.0 collective-permute-done.9.a_ref.rest_0_
  66.0 0.1 collective-permute-start.14
  66.1 1.6 %collective-permute-start.10 = (bf16[2,272,128]{2,1,0:T(8,128)(2,1)S(1)}, bf16[2,272,128]{2,1,0:T(8,128)(2,1)S(1)}, u32[]{:S(2)}, u32[]{:S(2)}) collective-permute-start(bf16[2,272,128]{2,1,0:T(8,128)(2,1)S(1)} %collective-permute-done.9.a_ref.rest_0_), channel_id=1, source_target_pairs={{0,2},{1,3},{2,0},{3,1},{4,6},{5,7},{6,4},{7,5},{8,10},{9,11},{10,... | collective-permute-start | bytes 417800 | tf_op jit(solution)/shard_map/ppermute | solution.py:658
  67.6 0.2 collective-permute-start.13
  67.8 4.4 %collective-permute-done.10.rest_0_ = bf16[2,272,128]{2,1,0:T(8,128)(2,1)S(1)} collective-permute-done((bf16[2,272,128]{2,1,0:T(8,128)(2,1)S(1)}, bf16[2,272,128]{2,1,0:T(8,128)(2,1)S(1)}, u32[]{:S(2)}, u32[]{:S(2)}) %collective-permute-start.10) | collective-permute-done | bytes 139296 | tf_op jit(solution)/shard_map/ppermute | solution.py:658
  72.2 0.0 collective-permute-start.11
  72.2 4.9 %shard_map.202 = (f32[64,512]{1,0:T(8,128)S(1)}, f32[64,512]{1,0:T(8,128)S(1)}, f32[16,128]{1,0:T(8,128)S(1)}, bf16[1,3,512,512]{3,2,1,0:T(8,128)(2,1)S(1)}, bf1...) custom-call(s32[1]{0:T(128)} %bitcast.me_ref, ...), custom_call_target="tpu_custom_call" | custom-call | tf_op jit(solution)/shard_map/pallas_call | solution.py:40
  77.1 0.8 shard_map.203
  77.9 0.0 collective-permute-done.11.rest_0_
  78.0 0.8 shard_map.204.x_ref.token_ref
  78.8 2.1 %shard_map.205 = (bf16[4,64,512]{2,1,0:T(8,128)(2,1)S(1)}, bf16[4,64,512]{2,1,0:T(8,128)(2,1)S(1)}) custom-call(f32[2,4]{1,0:T(2,128)S(1)} %copy-done, bf16[64,512]{1,0:T(8,128)(2,1)S(1)} %shard_map.204.x_ref.token_ref, bf16[64,512]{1,0:T(8,128)(2,1)S(1)} %shard_map.204.x_ref.token_ref, bf16[1,2,512,512]{3,2,1,0:T(8,128)(2,1)S(1)} %get-tuple-element.167.rest_0_, ...), custom_call_target="tpu_custom_call" | custom-call | tf_op jit(solution)/shard_map/pallas_call | solution.py:40
  80.9 0.4 collective-permute-start.15
  81.3 0.1 collective-permute-start.16
  81.4 1.7 %shard_map.206.keep_ref = bf16[4,64,512]{2,1,0:T(8,128)(2,1)S(1)} custom-call(f32[2,4]{1,0:T(2,128)S(1)} %copy-done, bf16[64,512]{1,0:T(8,128)(2,1)S(1)} %shard_map.204.x_ref.token_ref, bf16[4,64,512]{2,1,0:T(8,128)(2,1)S(1)} %get-tuple-element.175.token_ref, bf16[1,3,512,512]{3,2,1,0:T(8,128)(2,1)S(1)} %get-tuple-element.176.rest_0_, ...), custom_call_target="tpu_custom_call" | custom-call | tf_op jit(solution)/shard_map/pallas_call | solution.py:40
  83.2 0.1 shard_map.207
  83.2 1.6 %collective-permute-start.18 = (bf16[2,64,512]{2,1,0:T(8,128)(2,1)S(1)}, bf16[2,64,512]{2,1,0:T(8,128)(2,1)S(1)}, u32[]{:S(2)}, u32[]{:S(2)}) collective-permute-start(bf16[2,64,512]{2,1,0:T(8,128)(2,1)S(1)} %get-tuple-element.181.token_ref), channel_id=1, source_target_pairs={{0,2},{1,3},{2,0},{3,1},{4,6},{5,7},{6,4},{7,5},{8,10},{9,11},{10,... | collective-permute-start | bytes 393224 | tf_op jit(solution)/shard_map/ppermute | solution.py:658
  84.8 0.5 collective-permute-start.17
  85.3 1.7 %shard_map.208.keep_ref = bf16[4,64,512]{2,1,0:T(8,128)(2,1)S(1)} custom-call(f32[2,4]{1,0:T(2,128)S(1)} %copy-done, bf16[64,512]{1,0:T(8,128)(2,1)S(1)} %shard_map.204.x_ref.token_ref, bf16[2,64,512]{2,1,0:T(8,128)(2,1)S(1)} %get-tuple-element.181.token_ref, bf16[1,3,512,512]{3,2,1,0:T(8,128)(2,1)S(1)} %get-tuple-element.182.rest_0_, ...), custom_call_target="tpu_custom_call" | custom-call | tf_op jit(solution)/shard_map/pallas_call | solution.py:40
  87.1 0.1 shard_map.209
  87.1 2.5 %collective-permute-done.18.got_ref = bf16[2,64,512]{2,1,0:T(8,128)(2,1)S(1)} collective-permute-done((bf16[2,64,512]{2,1,0:T(8,128)(2,1)S(1)}, bf16[2,64,512]{2,1,0:T(8,128)(2,1)S(1)}, u32[]{:S(2)}, u32[]{:S(2)}) %collective-permute-start.18) | collective-permute-done | bytes 131104 | tf_op jit(solution)/shard_map/ppermute | solution.py:658
  89.7 1.4 %collective-permute-start.19 = (bf16[2,64,512]{2,1,0:T(8,128)(2,1)S(1)}, bf16[2,64,512]{2,1,0:T(8,128)(2,1)S(1)}, u32[]{:S(2)}, u32[]{:S(2)}) collective-permute-start(bf16[2,64,512]{2,1,0:T(8,128)(2,1)S(1)} %shard_map.211), channel_id=1, source_target_pairs={{0,4},{1,5},{2,6},{3,7},{4,0},{5,1},{6,2},{7,3},{8,12},{9,13},{10,... | collective-permute-start | bytes 393224 | tf_op jit(solution)/shard_map/ppermute | solution.py:658
  91.1 0.8 collective-permute-done.17.got_ref
  92.0 2.8 %collective-permute-done.19.got_ref = bf16[2,64,512]{2,1,0:T(8,128)(2,1)S(1)} collective-permute-done((bf16[2,64,512]{2,1,0:T(8,128)(2,1)S(1)}, bf16[2,64,512]{2,1,0:T(8,128)(2,1)S(1)}, u32[]{:S(2)}, u32[]{:S(2)}) %collective-permute-start.19) | collective-permute-done | bytes 131104 | tf_op jit(solution)/shard_map/ppermute | solution.py:658
  94.8 1.9 %collective-permute-start.20 = (bf16[1,64,512]{2,1,0:T(8,128)(2,1)S(1)}, bf16[1,64,512]{2,1,0:T(8,128)(2,1)S(1)}, u32[]{:S(2)}, u32[]{:S(2)}) collective-permute-start(bf16[1,64,512]{2,1,0:T(8,128)(2,1)S(1)} %get-tuple-element.190), channel_id=1, source_target_pairs={{0,8},{1,9},{2,10},{3,11},{4,12},{5,13},{6,14},{7,15},{8,0},{9,1},... | collective-permute-start | bytes 196616 | tf_op jit(solution)/shard_map/ppermute | solution.py:658
  96.7 3.3 %collective-permute-done.20.got_ref = bf16[1,64,512]{2,1,0:T(8,128)(2,1)S(1)} collective-permute-done((bf16[1,64,512]{2,1,0:T(8,128)(2,1)S(1)}, bf16[1,64,512]{2,1,0:T(8,128)(2,1)S(1)}, u32[]{:S(2)}, u32[]{:S(2)}) %collective-permute-start.20) | collective-permute-done | bytes 65568 | tf_op jit(solution)/shard_map/ppermute | solution.py:658
  100.0 0.6 collective-permute-start.21
  100.6 3.8 %collective-permute-done.21.got_ref = bf16[1,64,512]{2,1,0:T(8,128)(2,1)S(1)} collective-permute-done((bf16[1,64,512]{2,1,0:T(8,128)(2,1)S(1)}, bf16[1,64,512]{2,1,0:T(8,128)(2,1)S(1)}, u32[]{:S(2)}, u32[]{:S(2)}) %collective-permute-start.21) | collective-permute-done | bytes 65568 | tf_op jit(solution)/shard_map/ppermute | solution.py:661
  104.4 0.8 shard_map.214
  (18 shorter events, 0.2 us)
Async XLA Ops:
  0.0 0.7 copy-start.1
  0.7 7.5 %copy-start = (f32[2,4]{1,0:T(2,128)S(1)}, f32[2,4]{1,0:T(2,128)}, u32[]{:S(2)}) copy-start(f32[2,4]{1,0:T(2,128)} %scale_ref.25) | copy-start | bytes 100
  7.6 3.4 %collective-permute-start = (bf16[8,144,128]{2,1,0:T(8,128)(2,1)S(1)}, bf16[8,144,128]{2,1,0:T(8,128)(2,1)S(1)}, u32[]{:S(2)}, u32[]{:S(2)}) collective-permute-start(bf16[8,144,128]{2,1,0:T(8,128)(2,1)S(1)} %get-tuple-element.102.refs_0_), channel_id=1, source_target_pairs={{0,1},{1,0},{2,3},{3,2},{4,5},{5,4},{6,7},{7,6},{8,9},{9,8},{10,11... | collective-permute-start | bytes 884744 | tf_op jit(solution)/shard_map/ppermute | solution.py:658
  11.2 7.1 %collective-permute-start.1 = (bf16[4,144,128]{2,1,0:T(8,128)(2,1)S(1)}, bf16[4,144,128]{2,1,0:T(8,128)(2,1)S(1)}, u32[]{:S(2)}, u32[]{:S(2)}) collective-permute-start(bf16[4,144,128]{2,1,0:T(8,128)(2,1)S(1)} %get-tuple-element.105.refs_0_), channel_id=1, source_target_pairs={{0,2},{1,3},{2,0},{3,1},{4,6},{5,7},{6,4},{7,5},{8,10},{9,11},{10,... | collective-permute-start | bytes 442376 | tf_op jit(solution)/shard_map/ppermute | solution.py:658
  18.4 5.2 %collective-permute-start.2 = (bf16[2,144,128]{2,1,0:T(8,128)(2,1)S(1)}, bf16[2,144,128]{2,1,0:T(8,128)(2,1)S(1)}, u32[]{:S(2)}, u32[]{:S(2)}) collective-permute-start(bf16[2,144,128]{2,1,0:T(8,128)(2,1)S(1)} %get-tuple-element.108.refs_0_), channel_id=1, source_target_pairs={{0,4},{1,5},{2,6},{3,7},{4,0},{5,1},{6,2},{7,3},{8,12},{9,13},{10,... | collective-permute-start | bytes 221192 | tf_op jit(solution)/shard_map/ppermute | solution.py:658
  23.7 7.1 %collective-permute-start.3 = (bf16[2,144,128]{2,1,0:T(8,128)(2,1)S(1)}, bf16[2,144,128]{2,1,0:T(8,128)(2,1)S(1)}, u32[]{:S(2)}, u32[]{:S(2)}) collective-permute-start(bf16[2,144,128]{2,1,0:T(8,128)(2,1)S(1)} %shard_map.187.refs_0_.own_ref), channel_id=1, source_target_pairs={{0,8},{1,9},{2,10},{3,11},{4,12},{5,13},{6,14},{7,15},{8,0},{9,1},... | collective-permute-start | bytes 221192 | tf_op jit(solution)/shard_map/ppermute | solution.py:658
  31.0 4.4 %collective-permute-start.4 = (bf16[2,128,128]{2,1,0:T(8,128)(2,1)S(1)}, bf16[2,128,128]{2,1,0:T(8,128)(2,1)S(1)}, u32[]{:S(2)}, u32[]{:S(2)}) collective-permute-start(bf16[2,128,128]{2,1,0:T(8,128)(2,1)S(1)} %shard_map.189.refs_0_.a_ref), channel_id=1, source_target_pairs={{0,4},{1,5},{2,6},{3,7},{4,0},{5,1},{6,2},{7,3},{8,12},{9,13},{10,... | collective-permute-start | bytes 196616 | tf_op jit(solution)/shard_map/ppermute | solution.py:658
  35.4 6.4 %collective-permute-start.5 = (bf16[4,128,128]{2,1,0:T(8,128)(2,1)S(1)}, bf16[4,128,128]{2,1,0:T(8,128)(2,1)S(1)}, u32[]{:S(2)}, u32[]{:S(2)}) collective-permute-start(bf16[4,128,128]{2,1,0:T(8,128)(2,1)S(1)} %shard_map.191.refs_0_.a_ref), channel_id=1, source_target_pairs={{0,2},{1,3},{2,0},{3,1},{4,6},{5,7},{6,4},{7,5},{8,10},{9,11},{10,... | collective-permute-start | bytes 393224 | tf_op jit(solution)/shard_map/ppermute | solution.py:658
  41.8 1.6 %collective-permute-start.6 = (bf16[8,128,128]{2,1,0:T(8,128)(2,1)S(1)}, bf16[8,128,128]{2,1,0:T(8,128)(2,1)S(1)}, u32[]{:S(2)}, u32[]{:S(2)}) collective-permute-start(bf16[8,128,128]{2,1,0:T(8,128)(2,1)S(1)} %shard_map.193.low_ref), channel_id=1, source_target_pairs={{0,1},{1,0},{2,3},{3,2},{4,5},{5,4},{6,7},{7,6},{8,9},{9,8},{10,11... | collective-permute-start | bytes 786440 | tf_op jit(solution)/shard_map/ppermute | solution.py:658
  46.3 6.0 %collective-permute-start.7 = (bf16[64,512]{1,0:T(8,128)(2,1)S(1)}, bf16[64,512]{1,0:T(8,128)(2,1)S(1)}, u32[]{:S(2)}, u32[]{:S(2)}) collective-permute-start(bf16[64,512]{1,0:T(8,128)(2,1)S(1)} %shard_map.194.refs_0_.own_ref), channel_id=1, source_target_pairs={{0,16},{16,0},{1,17},{17,1},{2,18},{18,2},{3,19},{19,3},{4,20},{20... | collective-permute-start | bytes 196616 | tf_op jit(solution)/shard_map/ppermute | solution.py:661
  52.5 6.4 %collective-permute-start.8 = (bf16[1,272,128]{2,1,0:T(8,128)(2,1)S(1)}, bf16[1,272,128]{2,1,0:T(8,128)(2,1)S(1)}, u32[]{:S(2)}, u32[]{:S(2)}) collective-permute-start(bf16[1,272,128]{2,1,0:T(8,128)(2,1)S(1)} %get-tuple-element.123.refs_0_.a_ref), channel_id=1, source_target_pairs={{0,8},{1,9},{2,10},{3,11},{4,12},{5,13},{6,14},{7,15},{8,0},{9,1},... | collective-permute-start | bytes 208904 | tf_op jit(solution)/shard_map/ppermute | solution.py:658
  58.9 7.0 %collective-permute-start.12 = (bf16[2,272,128]{2,1,0:T(8,128)(2,1)S(1)}, bf16[2,272,128]{2,1,0:T(8,128)(2,1)S(1)}, u32[]{:S(2)}, u32[]{:S(2)}) collective-permute-start(bf16[2,272,128]{2,1,0:T(8,128)(2,1)S(1)} %shard_map.198.refs_0_.rest_0_), channel_id=1, source_target_pairs={{0,2},{1,3},{2,0},{3,1},{4,6},{5,7},{6,4},{7,5},{8,10},{9,11},{10,... | collective-permute-start | bytes 417800 | tf_op jit(solution)/shard_map/ppermute | solution.py:658
  59.5 6.4 %collective-permute-start.9 = (bf16[2,272,128]{2,1,0:T(8,128)(2,1)S(1)}, bf16[2,272,128]{2,1,0:T(8,128)(2,1)S(1)}, u32[]{:S(2)}, u32[]{:S(2)}) collective-permute-start(bf16[2,272,128]{2,1,0:T(8,128)(2,1)S(1)} %shard_map.198.refs_0_.rest_0_), channel_id=1, source_target_pairs={{0,4},{1,5},{2,6},{3,7},{4,0},{5,1},{6,2},{7,3},{8,12},{9,13},{10,... | collective-permute-start | bytes 417800 | tf_op jit(solution)/shard_map/ppermute | solution.py:658
  66.0 6.2 %collective-permute-start.14 = (bf16[4,272,128]{2,1,0:T(8,128)(2,1)S(1)}, bf16[4,272,128]{2,1,0:T(8,128)(2,1)S(1)}, u32[]{:S(2)}, u32[]{:S(2)}) collective-permute-start(bf16[4,272,128]{2,1,0:T(8,128)(2,1)S(1)} %shard_map.201), channel_id=1, source_target_pairs={{0,1},{1,0},{2,3},{3,2},{4,5},{5,4},{6,7},{7,6},{8,9},{9,8},{10,11... | collective-permute-start | bytes 835592 | tf_op jit(solution)/shard_map/ppermute | solution.py:658
  66.1 6.1 %collective-permute-start.10 = (bf16[2,272,128]{2,1,0:T(8,128)(2,1)S(1)}, bf16[2,272,128]{2,1,0:T(8,128)(2,1)S(1)}, u32[]{:S(2)}, u32[]{:S(2)}) collective-permute-start(bf16[2,272,128]{2,1,0:T(8,128)(2,1)S(1)} %collective-permute-done.9.a_ref.rest_0_), channel_id=1, source_target_pairs={{0,2},{1,3},{2,0},{3,1},{4,6},{5,7},{6,4},{7,5},{8,10},{9,11},{10,... | collective-permute-start | bytes 417800 | tf_op jit(solution)/shard_map/ppermute | solution.py:658
  67.6 4.5 %collective-permute-start.13 = (bf16[2,272,128]{2,1,0:T(8,128)(2,1)S(1)}, bf16[2,272,128]{2,1,0:T(8,128)(2,1)S(1)}, u32[]{:S(2)}, u32[]{:S(2)}) collective-permute-start(bf16[2,272,128]{2,1,0:T(8,128)(2,1)S(1)} %shard_map.198.refs_0_.rest_0_), channel_id=1, source_target_pairs={{0,1},{1,0},{2,3},{3,2},{4,5},{5,4},{6,7},{7,6},{8,9},{9,8},{10,11... | collective-permute-start | bytes 417800 | tf_op jit(solution)/shard_map/ppermute | solution.py:658
  72.2 5.8 %collective-permute-start.11 = (bf16[2,272,128]{2,1,0:T(8,128)(2,1)S(1)}, bf16[2,272,128]{2,1,0:T(8,128)(2,1)S(1)}, u32[]{:S(2)}, u32[]{:S(2)}) collective-permute-start(bf16[2,272,128]{2,1,0:T(8,128)(2,1)S(1)} %collective-permute-done.10.rest_0_), channel_id=1, source_target_pairs={{0,1},{1,0},{2,3},{3,2},{4,5},{5,4},{6,7},{7,6},{8,9},{9,8},{10,11... | collective-permute-start | bytes 417800 | tf_op jit(solution)/shard_map/ppermute | solution.py:658
  80.9 2.3 %collective-permute-start.15 = (bf16[4,64,512]{2,1,0:T(8,128)(2,1)S(1)}, bf16[4,64,512]{2,1,0:T(8,128)(2,1)S(1)}, u32[]{:S(2)}, u32[]{:S(2)}) collective-permute-start(bf16[4,64,512]{2,1,0:T(8,128)(2,1)S(1)} %get-tuple-element.180), channel_id=1, source_target_pairs={{0,1},{1,0},{2,3},{3,2},{4,5},{5,4},{6,7},{7,6},{8,9},{9,8},{10,11... | collective-permute-start | bytes 786440 | tf_op jit(solution)/shard_map/ppermute | solution.py:658
  81.3 5.7 %collective-permute-start.16 = (bf16[4,64,512]{2,1,0:T(8,128)(2,1)S(1)}, bf16[4,64,512]{2,1,0:T(8,128)(2,1)S(1)}, u32[]{:S(2)}, u32[]{:S(2)}) collective-permute-start(bf16[4,64,512]{2,1,0:T(8,128)(2,1)S(1)} %get-tuple-element.175.token_ref), channel_id=1, source_target_pairs={{0,1},{1,0},{2,3},{3,2},{4,5},{5,4},{6,7},{7,6},{8,9},{9,8},{10,11... | collective-permute-start | bytes 786440 | tf_op jit(solution)/shard_map/ppermute | solution.py:658
  83.2 6.4 %collective-permute-start.18 = (bf16[2,64,512]{2,1,0:T(8,128)(2,1)S(1)}, bf16[2,64,512]{2,1,0:T(8,128)(2,1)S(1)}, u32[]{:S(2)}, u32[]{:S(2)}) collective-permute-start(bf16[2,64,512]{2,1,0:T(8,128)(2,1)S(1)} %get-tuple-element.181.token_ref), channel_id=1, source_target_pairs={{0,2},{1,3},{2,0},{3,1},{4,6},{5,7},{6,4},{7,5},{8,10},{9,11},{10,... | collective-permute-start | bytes 393224 | tf_op jit(solution)/shard_map/ppermute | solution.py:658
  84.8 7.1 %collective-permute-start.17 = (bf16[2,64,512]{2,1,0:T(8,128)(2,1)S(1)}, bf16[2,64,512]{2,1,0:T(8,128)(2,1)S(1)}, u32[]{:S(2)}, u32[]{:S(2)}) collective-permute-start(bf16[2,64,512]{2,1,0:T(8,128)(2,1)S(1)} %get-tuple-element.187), channel_id=1, source_target_pairs={{0,2},{1,3},{2,0},{3,1},{4,6},{5,7},{6,4},{7,5},{8,10},{9,11},{10,... | collective-permute-start | bytes 393224 | tf_op jit(solution)/shard_map/ppermute | solution.py:658
  89.7 5.0 %collective-permute-start.19 = (bf16[2,64,512]{2,1,0:T(8,128)(2,1)S(1)}, bf16[2,64,512]{2,1,0:T(8,128)(2,1)S(1)}, u32[]{:S(2)}, u32[]{:S(2)}) collective-permute-start(bf16[2,64,512]{2,1,0:T(8,128)(2,1)S(1)} %shard_map.211), channel_id=1, source_target_pairs={{0,4},{1,5},{2,6},{3,7},{4,0},{5,1},{6,2},{7,3},{8,12},{9,13},{10,... | collective-permute-start | bytes 393224 | tf_op jit(solution)/shard_map/ppermute | solution.py:658
  94.8 5.2 %collective-permute-start.20 = (bf16[1,64,512]{2,1,0:T(8,128)(2,1)S(1)}, bf16[1,64,512]{2,1,0:T(8,128)(2,1)S(1)}, u32[]{:S(2)}, u32[]{:S(2)}) collective-permute-start(bf16[1,64,512]{2,1,0:T(8,128)(2,1)S(1)} %get-tuple-element.190), channel_id=1, source_target_pairs={{0,8},{1,9},{2,10},{3,11},{4,12},{5,13},{6,14},{7,15},{8,0},{9,1},... | collective-permute-start | bytes 196616 | tf_op jit(solution)/shard_map/ppermute | solution.py:658
  100.0 4.3 %collective-permute-start.21 = (bf16[1,64,512]{2,1,0:T(8,128)(2,1)S(1)}, bf16[1,64,512]{2,1,0:T(8,128)(2,1)S(1)}, u32[]{:S(2)}, u32[]{:S(2)}) collective-permute-start(bf16[1,64,512]{2,1,0:T(8,128)(2,1)S(1)} %shard_map.213.own_ref), channel_id=1, source_target_pairs={{0,16},{16,0},{1,17},{17,1},{2,18},{18,2},{3,19},{19,3},{4,20},{20... | collective-permute-start | bytes 196616 | tf_op jit(solution)/shard_map/ppermute | solution.py:661
where the time goes:
time: 105 us
  Pallas kernels  61.5 us (59%)
  starting transfers between devices  23.3 us (22%)
  waiting for transfers between devices  19.5 us (19%)
    pallas_call x34, Pallas kernels, call(): pl.pallas_call(kernel, in_specs=[IN_SMEM] * len(scalars) + [IN_VMEM] * le...  61.5 us
    ppermute x20, starting transfers between devices, swap(): return lax.ppermute(x, 'ctx', [(i, i ^ 1 << bit) for i in range(n)])  21.1 us
    ppermute x20, waiting for transfers between devices, swap(): return lax.ppermute(x, 'ctx', [(i, i ^ 1 << bit) for i in range(n)])  15.7 us
    ppermute x2, waiting for transfers between devices, swap_kv(): return lax.ppermute(x, 'kv', [(i, (i + 1) % n_kv) for i in range(n_kv)])  3.77 us
    ppermute x2, starting transfers between devices, swap_kv(): return lax.ppermute(x, 'kv', [(i, (i + 1) % n_kv) for i in range(n_kv)])  2.14 us
  transfers between devices with their start and end apart: 22, of which 9 were waited for; matrix products, arithmetic and copies ran while one was open for 0% of the time, Pallas kernels for 45%

commit v1 on v0

v1 whole, which is shorter than its diff:
```python
import functools

import jax
import jax.numpy as jnp
from jax import lax
from jax.experimental import pallas as pl
from jax.experimental.pallas import tpu as pltpu
from jax.sharding import PartitionSpec as P

HEAD_SIZE = 128
LANES = 128
STAT_ROWS = 16
NEG = -1e30
EPS = 1e-05
LOG2E = 1.4426950408889634
MIB = 1 << 20
F32 = jnp.float32
BF16 = jnp.bfloat16


IN_VMEM = pl.BlockSpec(memory_space=pltpu.VMEM)
IN_HBM = pl.BlockSpec(memory_space=pl.ANY)


def vmem(x):
    return pltpu.with_memory_space_constraint(x, pltpu.VMEM)


def hbm(x):
    return pltpu.with_memory_space_constraint(x, pltpu.HBM)


def call(kernel, arrays, shapes, far=(), scratch=(), limit=MIB, far_out=False):
    if far_out:
        out_shape = [jax.ShapeDtypeStruct(s, d) for s, d in shapes]
    else:
        out_shape = [pltpu.VMEM(s, d) for s, d in shapes]
    return pl.pallas_call(
        kernel,
        in_specs=[IN_VMEM] * len(arrays) + [IN_HBM] * len(far),
        out_specs=[IN_VMEM] * len(shapes),
        out_shape=out_shape,
        scratch_shapes=list(scratch),
        compiler_params=pltpu.CompilerParams(vmem_limit_bytes=limit),
    )(*[vmem(a) for a in arrays], *[hbm(a) for a in far])


def my_place():
    return lax.axis_index("ctx").astype(jnp.int32)


def scales_of(scale_ref, kind, factor):
    return [scale_ref[t : t + 1, kind : kind + 1] * factor for t in range(scale_ref.shape[0])]


def iota(shape, dim):
    return lax.broadcasted_iota(jnp.int32, shape, dim)


def to_row(column):
    rows = column.shape[0]
    diagonal = iota((rows, LANES), 0) == iota((rows, LANES), 1)
    return jnp.sum(jnp.where(diagonal, column, 0.0), axis=0, keepdims=True)


def to_column(row, rows):
    diagonal = iota((rows, LANES), 0) == iota((rows, LANES), 1)
    return jnp.sum(jnp.where(diagonal, row, 0.0), axis=1, keepdims=True)


def pack_row(row):
    high = row.astype(BF16).astype(F32)
    middle = (row - high).astype(BF16).astype(F32)
    low = row - high - middle
    place = iota((STAT_ROWS, LANES), 0)
    packed = jnp.where(place == 0, high, jnp.where(place == 1, middle, low))
    return jnp.where(place < 3, packed, 0.0).astype(BF16)


def unpack_row(block):
    return jnp.sum(block.astype(F32), axis=0, keepdims=True)


def reversed_bits(value, bits):
    out = 0
    for i in range(bits):
        out = out | (((value >> i) & 1) << (bits - 1 - i))
    return out


def start_halves(copies, rows):
    def half(h, carry):
        for copy in copies(pl.multiple_of(h * (rows // 2), rows // 2), rows // 2):
            copy.start()
        return carry

    lax.fori_loop(0, 2, half, 0)


def attention_kernel(bits, loads, n_sources, *refs):
    me = my_place()
    ids_hbm, tree_hbm, q_hbm, dk_hbm, dv_hbm, k_hbm, v_hbm, len_hbm, res_hbm, gain_hbm = refs[:10]
    sources, refs = refs[10 : 10 + 2 * n_sources], refs[10 + 2 * n_sources :]
    keep_ref, send_ref, pm_ref, res_ref, gain_ref = refs[:5]
    raw_refs, refs = refs[5 : 5 + len(loads)], refs[5 + len(loads) :]
    ids_ref, tree_ref, q_ref, dk_ref, dv_ref, k_ref, v_ref, len_ref, sems, raw_sems = refs
    tenants, slots, _ = k_ref.shape
    small = [
        pltpu.make_async_copy(source, target, sems.at[i])
        for i, (source, target) in enumerate(
            [
                (ids_hbm, ids_ref), (tree_hbm, tree_ref), (q_hbm, q_ref), (dk_hbm, dk_ref),
                (dv_hbm, dv_ref), (len_hbm, len_ref), (res_hbm, res_ref), (gain_hbm, gain_ref),
            ]
        )
    ]
    cache = []
    for t in range(tenants):
        at = len(small) + 2 * t
        cache.append(
            [
                pltpu.make_async_copy(k_hbm.at[t], k_ref.at[t], sems.at[at]),
                pltpu.make_async_copy(v_hbm.at[t], v_ref.at[t], sems.at[at + 1]),
            ]
        )
    raw_copies, raw_rows = raw_copies_of(loads, me, bits, sources, raw_refs, raw_sems)
    for copy in small + [c for pair in cache for c in pair]:
        copy.start()
    start_halves(raw_copies, raw_rows)

    tokens = tree_ref.shape[0]
    draft = tokens // tenants
    groups = dk_ref.shape[1] // HEAD_SIZE
    width = q_ref.shape[1] // dk_ref.shape[1]
    core = me & 1
    rows = keep_ref.shape[1] - STAT_ROWS
    parts = width * draft // rows
    factor = HEAD_SIZE ** (-0.5)
    power = factor * LOG2E
    nt = (((1,), (1,)), ((), ()))

    for copy in small:
        copy.wait()
    a = iota((tokens, tokens), 0)
    b = iota((tokens, tokens), 1)
    across = jnp.broadcast_to(ids_ref[...], (tokens, tokens))
    along = jnp.sum(jnp.where(a == b, across, 0), axis=1, keepdims=True)
    before = (along < across) | ((along == across) & (a < b))
    place = jnp.sum(before.astype(jnp.int32), axis=0, keepdims=True)
    choose = (place == a).astype(F32).astype(BF16)
    pm_ref[...] = choose
    seen_all = jnp.dot(choose, tree_ref[...].astype(F32).astype(BF16), preferred_element_type=F32)
    seen_all = jnp.where(me == 0, seen_all, 0.0)
    mine = jnp.dot(choose, q_ref[...], preferred_element_type=F32).astype(BF16)

    for t in range(tenants):
        seen = jnp.concatenate([seen_all[t * draft : (t + 1) * draft]] * width, axis=0) > 0.5
        live = me * slots + iota((1, slots), 1) < len_ref[t]
        for copy in cache[t]:
            copy.wait()
        for g in range(groups):
            head = slice(g * HEAD_SIZE, (g + 1) * HEAD_SIZE)
            query = jnp.concatenate(
                [
                    mine[
                        t * draft : (t + 1) * draft,
                        (g * width + w) * HEAD_SIZE : (g * width + w + 1) * HEAD_SIZE,
                    ]
                    for w in range(width)
                ],
                axis=0,
            )
            far = lax.dot_general(query, k_ref[t, :, head], nt, preferred_element_type=F32)
            near = lax.dot_general(query, dk_ref[:, head], nt, preferred_element_type=F32)
            far = jnp.where(live, far, NEG)
            near = jnp.where(seen, near, NEG)
            peak = jnp.maximum(
                jnp.max(far, axis=1, keepdims=True), jnp.max(near, axis=1, keepdims=True)
            )
            some = peak > 0.5 * NEG
            far = jnp.exp2((far - peak) * power)
            near = jnp.exp2((near - peak) * power)
            total = jnp.sum(far, axis=1, keepdims=True) + jnp.sum(near, axis=1, keepdims=True)
            value = jnp.dot(far.astype(BF16), v_ref[t, :, head], preferred_element_type=F32)
            value = value + jnp.dot(near.astype(BF16), dv_ref[:, head], preferred_element_type=F32)
            value = value * (1.0 / total)
            level = jnp.where(some, peak * factor + jnp.log(total), NEG)
            for i in range(0, parts, 2):
                even = value[i * rows : (i + 1) * rows]
                odd = value[(i + 1) * rows : (i + 2) * rows]
                even_level = to_row(level[i * rows : (i + 1) * rows])
                odd_level = to_row(level[(i + 1) * rows : (i + 2) * rows])
                block = (t * groups + g) * parts + i
                where = reversed_bits((block >> 1) ^ (me >> 1), bits - 1)
                first = core == 0
                keep_ref[where, :rows, :] = jnp.where(first, even, odd).astype(BF16)
                send_ref[where, :rows, :] = jnp.where(first, odd, even).astype(BF16)
                keep_ref[where, rows:, :] = pack_row(jnp.where(first, even_level, odd_level))
                send_ref[where, rows:, :] = pack_row(jnp.where(first, odd_level, even_level))
    for copy in raw_copies(0, raw_rows):
        copy.wait()


def attention_partials(
    lengths, tenant_ids, tree, queries, dk, dv, keys, values, residual, gain, loads, sources, n
):
    tenants = keys.shape[0]
    tokens = tenant_ids.shape[0]
    groups = dk.shape[1] // HEAD_SIZE
    width = queries.shape[1] // dk.shape[1]
    rows = tokens * groups * width // n
    part = ((n // 2, rows + STAT_ROWS, HEAD_SIZE), BF16)
    gain = gain.reshape(1, gain.shape[0])
    ids = tenant_ids.reshape(1, tokens)
    inner = [ids, tree, queries, dk, dv, keys, values]
    loads, far = used_sources(loads, sources)
    return call(
        functools.partial(attention_kernel, n.bit_length() - 1, loads, len(far) // 2),
        [],
        [part, part, ((tokens, tokens), BF16), (residual.shape, BF16), (gain.shape, F32)]
        + [l.raw_shape(tenants) for l in loads],
        far=inner + [lengths, residual, gain] + far,
        scratch=[pltpu.VMEM(x.shape, x.dtype) for x in inner]
        + [
            pltpu.SMEM(lengths.shape, lengths.dtype),
            pltpu.SemaphoreType.DMA((8 + 2 * tenants,)),
            raw_semaphores(loads, tenants),
        ],
        limit=12 * MIB,
    )


def merged(a_ref, i, b_ref, j, rows):
    a = unpack_row(a_ref[i, rows:, :])
    b = unpack_row(b_ref[j, rows:, :])
    peak = jnp.maximum(a, b)
    ea = jnp.exp(a - peak)
    eb = jnp.exp(b - peak)
    total = ea + eb
    wa = to_column(ea / total, rows)
    mine = a_ref[i, :rows, :].astype(F32)
    value = b_ref[j, :rows, :].astype(F32)
    return (value + (mine - value) * wa).astype(BF16), peak + jnp.log(total)


def merge_kernel(keep_ref, got_ref, token_ref, *outs):
    count = got_ref.shape[0]
    rows = keep_ref.shape[1] - STAT_ROWS
    for i in range(count):
        value, level = merged(keep_ref, i, got_ref, i, rows)
        per_out = count // len(outs)
        out, j = outs[i // per_out], i % per_out
        out[j, :rows, :] = value
        out[j, rows:, :] = pack_row(level)


def merge(keep, got, token):
    count, tall, lanes = got.shape
    outs = 1 if count == 2 else 2
    shapes = [((count // outs, tall, lanes), BF16)] * outs
    return call(merge_kernel, [keep, got, token], shapes)


def finish_rows_kernel(own_ref, got_ref, token_ref, o_ref):
    rows = o_ref.shape[1]
    for i in range(2):
        o_ref[i] = merged(own_ref, i, got_ref, 1 - i, rows)[0]


def finish_rows(own, got, token):
    _, tall, lanes = own.shape
    return call(
        finish_rows_kernel, [own, got, token],
        [((2, tall - STAT_ROWS, lanes), BF16)],
    )[0]


def join_kernel(a_ref, b_ref, token_ref, o_ref):
    count = a_ref.shape[0]
    o_ref[:count] = a_ref[...]
    o_ref[count:] = b_ref[...]


def join(a, b, token):
    shape = (a.shape[0] + b.shape[0],) + a.shape[1:]
    return call(join_kernel, [a, b, token], [(shape, a.dtype)])[0]


class Load:
    def __init__(self, source, kind, scale, pieces, block_of, by_column, shape):
        self.source, self.kind, self.scale, self.pieces = source, kind, scale, pieces
        self.block_of, self.by_column, self.shape = block_of, by_column, shape

    def at(self, source):
        return Load(
            source, self.kind, self.scale, self.pieces, self.block_of, self.by_column, self.shape
        )

    def raw_shape(self, tenants):
        return ((self.pieces, 1 + tenants) + self.shape, BF16)

    def views(self, me, bits, w, s, first, count):
        rows, columns = self.shape
        for g in range(self.pieces):
            block = self.block_of(g, me, bits)
            if self.by_column:
                at = (
                    pl.ds(first, count),
                    pl.ds(pl.multiple_of(block * columns, columns), columns),
                )
            else:
                at = (pl.ds(pl.multiple_of(block * rows, rows) + first, count),)
            yield w.at[at], [s.at[(t,) + at] for t in range(s.shape[0])]


def in_order(start):
    return lambda g, me, bits: reversed_bits(start + g, bits) ^ me


def own_core_first(start, count):
    def block_of(g, me, bits):
        i, core = start + g, me & 1
        return 2 * i + core if i < count // 2 else 2 * i - count + 1 - core

    return block_of


def used_sources(loads, sources):
    used = sorted({l.source for l in loads})
    return [l.at(used.index(l.source)) for l in loads], [x for i in used for x in sources[i]]


def raw_semaphores(loads, tenants):
    return pltpu.SemaphoreType.DMA((len(loads), max(l.pieces for l in loads) * (1 + tenants)))


def raw_copies_of(loads, me, bits, sources, outs, sems):
    whole = min(l.shape[0] for l in loads)

    def copies(first, count):
        for i, (load, out) in enumerate(zip(loads, outs)):
            many = load.shape[0] // whole
            w, s = sources[2 * load.source], sources[2 * load.source + 1]
            k = 0
            views = load.views(me, bits, w, s, first * many, count * many)
            for g, (base, signs) in enumerate(views):
                for j, view in enumerate([base] + signs):
                    to = out.at[g, j, pl.ds(first * many, count * many)]
                    yield pltpu.make_async_copy(view, to, sems.at[i, k])
                    k += 1

    return copies, whole


def groups_of(folds):
    groups = []
    for load in folds:
        if load.kind == 2:
            groups[-1].append(load)
        else:
            groups.append([load])
    return groups


def place_of(folds, i):
    for group, loads in enumerate(groups_of(folds)):
        if i < len(loads):
            return group, i * loads[0].pieces
        i -= len(loads)


def load_kernel(bits, loads, folds, n_sources, n_tokens, tenants, scale_ref, *refs):
    refs = refs[n_tokens:]
    raw_refs, refs = refs[: len(folds)], refs[len(folds) :]
    sources, refs = refs[: 2 * n_sources], refs[2 * n_sources :]
    n_outs = len(groups_of(folds))
    outs, refs = refs[:n_outs], refs[n_outs:]
    new_refs, token_ref, sems = refs[: len(loads)], refs[len(loads)], refs[len(loads) + 1 :]
    token_ref[...] = jnp.zeros_like(token_ref)
    if loads:
        copies, rows = raw_copies_of(loads, my_place(), bits, sources, new_refs, sems[0])
        start_halves(copies, rows)
    for i, (load, raw) in enumerate(zip(folds, raw_refs)):
        group, first = place_of(folds, i)
        out = outs[group].at[pl.ds(first, load.pieces)]
        rows = load.shape[0]
        step = min(64, rows)
        scales = scales_of(scale_ref, load.kind, load.scale)
        scales = [jnp.broadcast_to(x, (step, load.shape[1])) for x in scales]

        def fold(k, carry, out=out, raw=raw, scales=scales, load=load, step=step):
            at = pl.ds(pl.multiple_of(k * step, step), step)
            for g in range(load.pieces):
                base = raw[g, 0, at, :].astype(F32)
                for t in range(tenants):
                    sign = raw[g, 1 + t, at, :].astype(F32)
                    out[g, t, at, :] = (base + scales[t] * sign).astype(BF16)
            return carry

        lax.fori_loop(0, rows // step, fold, 0)
    if loads:
        for copy in copies(0, min(l.shape[0] for l in loads)):
            copy.wait()


def load(scale, bits, loads, folds, raws, sources, tokens, tenants):
    loads, far = used_sources(loads, sources)
    groups = groups_of(folds)
    shapes = [
        ((sum(l.pieces for l in group), tenants) + group[0].shape, BF16) for group in groups
    ] + [l.raw_shape(tenants) for l in loads]
    *blocks, token = call(
        functools.partial(
            load_kernel, bits, loads, folds, len(far) // 2, len(tokens), tenants
        ),
        [scale] + tokens + raws,
        shapes + [((8, LANES), F32)],
        far=far,
        scratch=[raw_semaphores(loads, tenants)] if loads else [],
        limit=MIB,
    )
    return blocks[: len(groups)], blocks[len(groups) :], token


def weighted(x, block, piece, scales):
    tenants = len(scales)
    draft = x.shape[0] // tenants
    raw = block.shape[1] > tenants
    parts = [
        jnp.dot(
            x[t * draft : (t + 1) * draft], block[piece, raw + t], preferred_element_type=F32
        )
        for t in range(tenants)
    ]
    if not raw:
        return jnp.concatenate(parts, axis=0)
    base = jnp.dot(x, block[piece, 0], preferred_element_type=F32)
    return base + jnp.concatenate([scales[t] * parts[t] for t in range(tenants)], axis=0)


def out_kernel(
    bits, factor, last, n_jobs, loads, n_sources, scale_ref, rows_ref, *rest
):
    w_refs, rest = rest[:n_jobs], rest[n_jobs:]
    if last:
        before_ref, *rest = rest
    sources, rest = rest[: 2 * n_sources], rest[2 * n_sources :]
    o_ref, raw_refs, x_ref = rest[0], rest[1 : 1 + len(loads)], rest[1 + len(loads)]
    if loads:
        raw_copies, raw_rows = raw_copies_of(loads, my_place(), bits, sources, raw_refs, rest[-1])
        start_halves(raw_copies, raw_rows)
    half, _, _ = rows_ref.shape
    pieces, deep = w_refs[0].shape[0], w_refs[0].shape[2]
    tenants = scale_ref.shape[0]
    draft = o_ref.shape[0] // tenants
    me = my_place()
    scales = scales_of(scale_ref, 0, factor)
    chunks = 2 * half // tenants
    block_of = own_core_first(chunks // 2 if last else 0, chunks)
    for i in range(chunks // 2):
        for t in range(tenants):
            where = reversed_bits((t * chunks + block_of(i, me, bits)) ^ me, bits) & (half - 1)
            for h in range(deep // HEAD_SIZE):
                column = i * deep + h * HEAD_SIZE
                x_ref[t * draft : (t + 1) * draft, column : column + HEAD_SIZE] = rows_ref[
                    where, h * draft : (h + 1) * draft, :
                ]
    base, delta = 0.0, [0.0] * tenants
    for i in range(chunks // 2):
        job, piece = divmod(i, pieces)
        x = x_ref[:, i * deep : (i + 1) * deep]
        base = base + jnp.dot(x, w_refs[job][piece, 0], preferred_element_type=F32)
        for t in range(tenants):
            delta[t] = delta[t] + jnp.dot(
                x[t * draft : (t + 1) * draft], w_refs[job][piece, 1 + t],
                preferred_element_type=F32,
            )
    for t in range(tenants):
        own = slice(t * draft, (t + 1) * draft)
        total = base[own] + scales[t] * delta[t]
        if last:
            total = (total + before_ref[own, :]).astype(BF16)
        o_ref[own, :] = total
    if loads:
        for copy in raw_copies(0, raw_rows):
            copy.wait()


def out_projection(scale, factor, rows, weights, tokens, loads, sources, before=()):
    half = rows.shape[0]
    features = weights[0].shape[-1]
    depth = sum(w.shape[0] * w.shape[2] for w in weights)
    last = len(before) > 0
    tenants = scale.shape[0]
    loads, far = used_sources(loads, sources)
    own, *raw = call(
        functools.partial(
            out_kernel, (2 * half).bit_length() - 1, factor, last, len(weights), loads,
            len(far) // 2,
        ),
        [scale, rows] + weights + list(before),
        [((tokens, features), BF16 if last else F32)] + [l.raw_shape(tenants) for l in loads],
        far=far,
        scratch=[pltpu.VMEM((tokens, depth), BF16)]
        + ([raw_semaphores(loads, tenants)] if loads else []),
    )
    return own, raw


def hidden_kernel(pm_ref, residual_ref, gain_ref, own_ref, got_ref, token_ref, hidden_ref, send_ref):
    tokens = own_ref.shape[0]
    hidden = jnp.dot(pm_ref[...], residual_ref[...], preferred_element_type=F32) + (
        own_ref[...].astype(F32) + got_ref[...].astype(F32)
    )
    hidden_ref[...] = hidden
    scaled = (hidden * gain_ref[...]).astype(BF16)
    pieces = hidden.shape[1] // LANES
    for f in range(pieces):
        send_ref[0, f * tokens : (f + 1) * tokens, :] = scaled[:, f * LANES : (f + 1) * LANES]
    squares = jnp.sum(hidden * hidden, axis=1, keepdims=True)
    send_ref[0, pieces * tokens :, :] = pack_row(to_row(squares))


def hidden_block(pm, residual, gain, own, got, token):
    tokens, features = own.shape
    tall = features // LANES * tokens + STAT_ROWS
    return call(
        hidden_kernel,
        [pm, residual, gain, own, got, token],
        [((tokens, features), F32), ((1, tall, LANES), BF16)],
    )


def gate_up_kernel(
    first, last, bits, counts, n_jobs, loads, width, n_down, factor, scale_ref, *rest
):
    n_x = len(counts)
    x_refs, rest = rest[:n_x], rest[n_x + 1 :]
    pair_refs, rest = rest[:n_jobs], rest[n_jobs:]
    before = ()
    if not first:
        before, rest = rest[:3], rest[3:]
    down_refs, rest = rest[:n_down], rest[n_down:]
    if loads:
        w_hbm, s_hbm, *rest = rest
        *rest, sems = rest
        split = 3
        rest, raw_refs = rest[:split], rest[split:]

        raw_copies, raw_rows = raw_copies_of(
            loads, my_place(), bits, (w_hbm, s_hbm), raw_refs, sems
        )
        start_halves(raw_copies, raw_rows)
    tokens = rest[0].shape[0]
    pieces, tenants = pair_refs[0].shape[0] // 2, pair_refs[0].shape[1]
    draft = tokens // tenants
    columns = (x_refs[0].shape[1] - STAT_ROWS) // tokens
    squares = jnp.zeros((STAT_ROWS, LANES), F32) if first else before[2][...]
    for x_ref, count in zip(x_refs, counts):
        for i in range(count):
            squares = squares + x_ref[i, columns * tokens :, :].astype(F32)
    if last:
        norm = to_column(
            lax.rsqrt(jnp.sum(squares, axis=0, keepdims=True) / width + EPS), tokens
        )
    else:
        rest[2][...] = squares
    for t in range(tenants):
        own = slice(t * draft, (t + 1) * draft)
        sums = [0.0, 0.0] if first else [before[j][own, :] for j in range(2)]
        block = 0
        for x_ref, count in zip(x_refs, counts):
            for i in range(count):
                x = jnp.concatenate(
                    [
                        x_ref[i, f * tokens + t * draft : f * tokens + (t + 1) * draft, :]
                        for f in range(columns)
                    ],
                    axis=1,
                )
                job, piece = divmod(block, pieces)
                block += 1
                for j in range(2):
                    sums[j] = sums[j] + jnp.dot(
                        x, pair_refs[job][j * pieces + piece, t], preferred_element_type=F32
                    )
        if last:
            gate = sums[0] * norm[own]
            up = sums[1] * norm[own]
            rest[0][own, :] = (gate / (1.0 + jnp.exp(-gate)) * up).astype(BF16)
        else:
            rest[0][own, :] = sums[0]
            rest[1][own, :] = sums[1]
    if last:
        down_products(factor, scale_ref, rest[0][...], down_refs, rest[1:3])
    if loads:
        for copy in raw_copies(0, raw_rows):
            copy.wait()


def gate_up(
    scale, bits, xs, token, pairs, tokens, width, before=(), downs=(), factor=1.0,
    loads=(), source=(),
):
    units = pairs[0].shape[-1]
    last = len(downs) > 0
    if last:
        shape = (downs[0].shape[0] * len(downs) // 2, tokens, downs[0].shape[-1])
        shapes = [((tokens, units), BF16)] + [(shape, BF16)] * 2
    else:
        shapes = [((tokens, units), F32)] * 2 + [((STAT_ROWS, LANES), F32)]
    scratch = []
    if loads:
        tenants = source[1].shape[0]
        loads = tuple(l.at(0) for l in loads)
        shapes += [l.raw_shape(tenants) for l in loads]
        scratch = [raw_semaphores(loads, tenants)]
    counts = tuple(x.shape[0] for x in xs)
    out = call(
        functools.partial(
            gate_up_kernel, not before, last, bits, counts, len(pairs), loads, width, len(downs),
            factor,
        ),
        [scale] + list(xs) + [token] + pairs + list(before) + list(downs),
        shapes,
        far=source if loads else (),
        scratch=scratch,
    )
    return out[:3], out[3:]


def down_products(factor, scale_ref, x, w_refs, o_refs):
    pieces = w_refs[0].shape[0]
    scales = scales_of(scale_ref, 3, factor)
    per_out = o_refs[0].shape[0]
    for i in range(per_out * len(o_refs)):
        job, piece = divmod(i, pieces)
        total = weighted(x, w_refs[job], piece, scales)
        o_refs[i // per_out][i % per_out] = total.astype(BF16)


def down_kernel(factor, scale_ref, x_ref, token_ref, *rest):
    down_products(factor, scale_ref, x_ref[...], rest[:-1], rest[-1:])


def down(scale, factor, active, token, weights):
    features = weights[0].shape[-1]
    tokens = active.shape[0]
    shape = (weights[0].shape[0] * len(weights), tokens, features)
    return call(
        functools.partial(down_kernel, factor), [scale, active, token] + weights, [(shape, BF16)]
    )[0]


def add_kernel(keep_ref, got_ref, *outs):
    count = got_ref.shape[0]
    per_out = count // len(outs)
    for i in range(count):
        total = (keep_ref[i].astype(F32) + got_ref[i].astype(F32)).astype(BF16)
        outs[i // per_out][i % per_out] = total


def total_kernel(*refs):
    *parts, o_ref = refs
    total = parts[0][...].astype(F32)
    for part in parts[1:]:
        total = total + part[...].astype(F32)
    o_ref[...] = total.astype(BF16)


def total_of(parts):
    return call(total_kernel, parts, [(parts[0].shape, BF16)])[0]


def add(keep, got, outs):
    count, tokens, features = got.shape
    return call(add_kernel, [keep, got], [((count // outs, tokens, features), BF16)] * outs)


def finish_kernel(pm_ref, hidden_ref, own_ref, got_ref, o_ref):
    mixed = hidden_ref[...] + (own_ref[0].astype(F32) + got_ref[0].astype(F32))
    o_ref[...] = lax.dot_general(
        pm_ref[...], mixed.astype(BF16), (((0,), (0,)), ((), ())), preferred_element_type=F32
    ).astype(BF16)


def finish(pm, hidden, own, got):
    return call(finish_kernel, [pm, hidden, own, got], [(hidden.shape, BF16)], far_out=True)[0]


def layer(
    residual,
    queries,
    draft_token_keys,
    draft_token_values,
    cache_keys,
    cached_value_rows,
    tenant_ids,
    tree_mask,
    cache_lengths,
    out_weight,
    out_signs,
    norm_gain,
    gate_weight,
    up_weight,
    down_weight,
    gate_signs,
    up_signs,
    down_signs,
    delta_scale,
):
    n = lax.axis_size("ctx")
    bits = n.bit_length() - 1
    tokens = tenant_ids.shape[0]
    tenants = cache_keys.shape[0]
    features = residual.shape[1]
    all_features, units = gate_weight.shape
    n_kv = lax.axis_size("kv")
    out_factor = (out_weight.shape[0] * n_kv) ** (-0.5)
    unit_factor = all_features ** (-0.5)
    down_factor = (units * n * n_kv) ** (-0.5)
    scale = delta_scale

    def swap(x, bit):
        return lax.ppermute(x, "ctx", [(i, i ^ (1 << bit)) for i in range(n)])

    def swap_kv(x):
        return lax.ppermute(x, "kv", [(i, (i + 1) % n_kv) for i in range(n_kv)])

    sources = [
        (gate_weight, gate_signs),
        (up_weight, up_signs),
        (down_weight, down_signs),
        (out_weight, out_signs),
    ]
    pieces = max(1, n // 16)
    eighth, quarter, half = n // 8, n // 4, n // 2
    todo = []
    spans = [(0, 3 * eighth), (half, 7 * eighth), (3 * eighth, half), (7 * eighth, n)]
    for i in [i for a, b in spans for i in range(a, b, pieces)]:
        shape = (features, units)
        at = in_order(i)
        todo.append((("gate", i), Load(0, 1, unit_factor, pieces, at, False, shape)))
        todo.append((("up", i), Load(1, 2, unit_factor, pieces, at, False, shape)))
    downs = [
        (("down", i), Load(2, 3, down_factor, pieces, in_order(i), True, (units, features)))
        for i in list(range(half, n, pieces)) + list(range(quarter, half, pieces))
        + list(range(0, quarter, pieces))
    ]
    todo += downs[:DOWN_EARLY]
    late, latest = downs[DOWN_EARLY:DOWN_LATE], downs[DOWN_LATE:]
    chunks = n // tenants
    outs = [
        Load(
            3, 0, out_factor, pieces, own_core_first(i, chunks), False,
            (out_weight.shape[0] // chunks, features),
        )
        for i in range(0, chunks, pieces)
    ]
    held, pending = {}, []

    def take(count):
        nonlocal todo
        now, todo = todo[:count], todo[count:]
        return now

    def keep_raw(now, raw):
        pending.extend(now)
        for (name, _), block in zip(now, raw):
            held[name] = block

    def fill(plan, *tokens_in):
        count, folds = plan
        now = take(count)
        old = pending[:folds]
        del pending[:folds]
        if not now and not old:
            return tokens_in[0]
        folded, raw, token = load(
            scale, bits, [l for _, l in now], [l for _, l in old],
            [held[name] for name, _ in old], sources, list(tokens_in), tenants,
        )
        firsts = [name for name, l in old if l.kind != 2]
        for name, block in zip(firsts, folded):
            held[name] = block
        keep_raw(now, raw)
        return token

    early = take(EARLY)
    keep, send, pm, residual_here, gain, *raw = attention_partials(
        cache_lengths, tenant_ids, tree_mask, queries, draft_token_keys, draft_token_values,
        cache_keys, cached_value_rows, residual, norm_gain, outs + [l for _, l in early],
        sources, n,
    )
    out_raw = raw[: len(outs)]
    keep_raw(early, raw[len(outs) :])
    plan = (PLAN_DOWN + [(0, 0)] * bits)[: bits - 1]
    for bit in range(bits - 1):
        got = swap(send, bit)
        token = fill(plan[bit], send)
        out = merge(keep, got, token)
        if bit < bits - 2:
            keep, send = out
    (both,) = out
    got = swap(both, bits - 1)
    token = fill(PLAN_TURN, both)
    rows = finish_rows(both, got, token)
    plan = ([(0, 0)] * bits + PLAN_UP)[-(bits - 2) :]
    for i, bit in enumerate(reversed(range(1, bits - 1))):
        got = swap(rows, bit)
        token = fill(plan[i], rows)
        rows = join(rows, got, token)
    other = swap(rows, 0)
    split = len(out_raw) // 2
    now = take(PLAN_OUT[0])
    own, raw = out_projection(
        scale, out_factor, rows, out_raw[:split], tokens, [l for _, l in now], sources
    )
    keep_raw(now, raw)
    now = take(PLAN_OUT[1])
    own, raw = out_projection(
        scale, out_factor, other, out_raw[split:], tokens, [l for _, l in now], sources,
        [own],
    )
    keep_raw(now, raw)

    got = swap_kv(own)
    token = fill(PLAN_LAST[0], own)
    hidden, block = hidden_block(pm, residual_here, gain, own, got, token)
    for bit in reversed(range(3, bits)):
        got = swap(block, bit)
        token = fill(PLAN_LAST[1], block)
        block = join(block, got, token)

    def gate_up_of(xs, spans, token, **options):
        names = [i for a, b in spans for i in range(a, b, pieces)]
        return gate_up(
            scale, bits, xs, token, [held["gate", i] for i in names],
            tokens, all_features, **options,
        )

    got_z = swap(block, 2)
    got_x = swap(block, 1)
    got_core = swap(block, 0)
    token = fill((len(todo), PLAN_LAST[2]), block)
    sums, _ = gate_up_of([block], [(0, eighth)], token)
    far_x = swap(got_z, 1)
    got_core_2 = swap(join(got_z, got_x, sums[2]), 0)
    sums, raw = gate_up_of(
        [got_z, got_x, got_core, got_core_2],
        [(eighth, 3 * eighth), (half, 7 * eighth)],
        sums[2],
        before=sums,
        loads=tuple(l for _, l in late),
        source=sources[2],
    )
    for (name, _), array in zip(late, raw):
        held[name] = array
    got_core_3 = swap(far_x, 0)
    sums, _ = gate_up_of([far_x], [(3 * eighth, half)], sums[2], before=sums)
    (active, send_near, send_far), raw = gate_up_of(
        [got_core_3],
        [(7 * eighth, n)],
        sums[2],
        before=sums,
        downs=[held["down", i] for i in range(half, n, pieces)],
        factor=down_factor,
        loads=tuple(l for _, l in latest),
        source=sources[2],
    )
    for (name, _), array in zip(latest, raw):
        held[name] = array

    def down_of(a, b, token):
        weights = [held["down", i] for i in range(a, b, pieces)]
        return down(scale, down_factor, active, token, weights)

    def swap_position(x, position):
        mask = reversed_bits(position, bits)
        return lax.ppermute(x, "ctx", [(i, i ^ mask) for i in range(n)])

    got_far = swap(send_far, 0)
    got_near = swap(send_near, 0)
    mine_far = down_of(quarter, half, send_near)
    x_late, x_early = add(mine_far, got_far, 2)
    got_early = swap(x_early, 1)
    got_late = swap(x_late, 1)
    mine_near = down_of(0, quarter, x_early)
    late_part, early_part = add(mine_near, got_near, 2)
    early_parts = add(early_part, got_early, eighth)
    arrived = [swap_position(x, eighth + i) for i, x in reversed(list(enumerate(early_parts)))]
    own, *late_parts = add(late_part, got_late, eighth)
    arrived += [swap_position(x, 1 + i) for i, x in reversed(list(enumerate(late_parts)))]
    total = total_of([own] + arrived)
    return finish(pm, hidden, total, swap_kv(total))


EARLY = 2
DOWN_EARLY = 8
DOWN_LATE = 12
PLAN_DOWN = [(0, 2), (7, 0), (3, 6)]
PLAN_TURN = (4, 4)
PLAN_UP = [(5, 4), (6, 4)]
PLAN_OUT = (0, 0)
PLAN_LAST = [(3, 6), (4, 4), 4]


def solution(mesh):
    return jax.shard_map(
        layer,
        mesh=mesh,
        in_specs=(
            P(None, "ctx"),
            P(None, "kv"),
            P(None, "kv"),
            P(None, "kv"),
            P(None, "ctx", "kv"),
            P(None, "ctx", "kv"),
            P(),
            P(),
            P(),
            P("kv", "ctx"),
            P(None, "kv", "ctx"),
            P("ctx"),
            P(None, ("kv", "ctx")),
            P(None, ("kv", "ctx")),
            P(("kv", "ctx"), None),
            P(None, None, ("kv", "ctx")),
            P(None, None, ("kv", "ctx")),
            P(None, ("kv", "ctx"), None),
            P(),
        ),
        out_specs=P(None, "ctx"),
        check_vma=False,
    )
```

time: 105 us -> 94.3 us (0.90)
  Pallas kernels: 61.5 us -> 49.4 us
  starting transfers between devices: 23.3 us -> 27.9 us
  waiting for transfers between devices: 19.5 us -> 16.5 us
    pallas_call x34 -> x33, Pallas kernels: 61.5 us -> 49.4 us  [call(): pl.pallas_call(kernel, in_specs=[IN_VMEM] * len(arrays) + [IN_HBM] * len(...]
    ppermute x20 -> x18, waiting for transfers between devices: 15.7 us -> 9.71 us  [swap(): return lax.ppermute(x, 'ctx', [(i, i ^ 1 << bit) for i in range(n)])]
    ppermute x0 -> x3, starting transfers between devices: none -> 5.52 us  [swap_position(): return lax.ppermute(x, 'ctx', [(i, i ^ mask) for i in range(n)])]
    ppermute x0 -> x3, waiting for transfers between devices: none -> 3.57 us  [swap_position(): return lax.ppermute(x, 'ctx', [(i, i ^ mask) for i in range(n)])]
    ppermute x20 -> x18, starting transfers between devices: 21.1 us -> 19.6 us  [swap(): return lax.ppermute(x, 'ctx', [(i, i ^ 1 << bit) for i in range(n)])]
  transfers between devices with their start and end apart: 22 -> 23, of which waited for: 9 -> 11; matrix products, arithmetic and copies ran while one was open for 0% -> 0% of each run, Pallas kernels for 45% -> 39%
where the time goes in v1:
time: 94.3 us; the launch traced here: 94.1 us
  Pallas kernels  49.4 us (52%)
  starting transfers between devices  27.9 us (30%)
  waiting for transfers between devices  16.5 us (17%)
    pallas_call x33, Pallas kernels, call(): pl.pallas_call(kernel, in_specs=[IN_VMEM] * len(arrays) + [IN_HBM] * len(...  49.4 us
    ppermute x18, starting transfers between devices, swap(): return lax.ppermute(x, 'ctx', [(i, i ^ 1 << bit) for i in range(n)])  19.6 us
    ppermute x18, waiting for transfers between devices, swap(): return lax.ppermute(x, 'ctx', [(i, i ^ 1 << bit) for i in range(n)])  9.71 us
    ppermute x3, starting transfers between devices, swap_position(): return lax.ppermute(x, 'ctx', [(i, i ^ mask) for i in range(n)])  5.52 us
    ppermute x3, waiting for transfers between devices, swap_position(): return lax.ppermute(x, 'ctx', [(i, i ^ mask) for i in range(n)])  3.57 us
    ppermute x2, waiting for transfers between devices, swap_kv(): return lax.ppermute(x, 'kv', [(i, (i + 1) % n_kv) for i in range(n_kv)])  3.2 us
    ppermute x2, starting transfers between devices, swap_kv(): return lax.ppermute(x, 'kv', [(i, (i + 1) % n_kv) for i in range(n_kv)])  2.77 us
  transfers between devices with their start and end apart: 23, of which 11 were waited for; matrix products, arithmetic and copies ran while one was open for 0% of the time, Pallas kernels for 39%

profile of v1, /device:TPU:0, one launch (start us, length us, event | category | flops | bytes accessed | tf_op | source)
XLA Modules:
  0.0 94.1 jit_solution(2112681212325880005)
XLA Ops:
  0.0 6.7 %shard_map.181 = (bf16[8,144,128]{2,1,0:T(8,128)(2,1)S(1)}, bf16[8,144,128]{2,1,0:T(8,128)(2,1)S(1)}, bf16[64,64]{1,0:T(8,128)(2,1)S(1)}, bf16[64,512]{1,0:T(8,1...) custom-call(s32[1,64]{1,0:T(1,128)} %bitcast.3, ...), custom_call_target="tpu_custom_call" | custom-call | tf_op jit(solution)/shard_map/pallas_call | solution.py:38
  6.7 0.6 collective-permute-start
  7.2 0.8 shard_map.182
  8.1 0.4 collective-permute-done.got_ref
  8.5 0.2 shard_map.183
  8.7 2.9 %collective-permute-start.1 = (bf16[4,144,128]{2,1,0:T(8,128)(2,1)S(1)}, bf16[4,144,128]{2,1,0:T(8,128)(2,1)S(1)}, u32[]{:S(2)}, u32[]{:S(2)}) collective-permute-start(bf16[4,144,128]{2,1,0:T(8,128)(2,1)S(1)} %get-tuple-element.128.refs_0_), channel_id=1, source_target_pairs={{0,2},{1,3},{2,0},{3,1},{4,6},{5,7},{6,4},{7,5},{8,10},{9,11},{10,... | collective-permute-start | bytes 442376 | tf_op jit(solution)/shard_map/ppermute | solution.py:725
  11.6 4.3 %shard_map.184 = (bf16[1,3,512,512]{3,2,1,0:T(8,128)(2,1)S(1)}, bf16[1,3,512,512]{3,2,1,0:T(8,128)(2,1)S(1)}, bf16[1,3,512,512]{3,2,1,0:T(8,128)(2,1)S(1)}, bf16...) custom-call(f32[2,4]{1,0:T(2,128)S(1)} %copy-done, ...), custom_call_target="tpu_custom_call" | custom-call | tf_op jit(solution)/shard_map/pallas_call | solution.py:38
  15.9 0.0 collective-permute-done.1.got_ref
  15.9 0.2 shard_map.185
  16.1 1.7 %collective-permute-start.2 = (bf16[2,144,128]{2,1,0:T(8,128)(2,1)S(1)}, bf16[2,144,128]{2,1,0:T(8,128)(2,1)S(1)}, u32[]{:S(2)}, u32[]{:S(2)}) collective-permute-start(bf16[2,144,128]{2,1,0:T(8,128)(2,1)S(1)} %get-tuple-element.131.refs_0_), channel_id=1, source_target_pairs={{0,4},{1,5},{2,6},{3,7},{4,0},{5,1},{6,2},{7,3},{8,12},{9,13},{10,... | collective-permute-start | bytes 221192 | tf_op jit(solution)/shard_map/ppermute | solution.py:725
  17.8 2.7 %shard_map.186 = (bf16[2,2,512,512]{3,2,1,0:T(8,128)(2,1)S(1)}, bf16[2,2,512,512]{3,2,1,0:T(8,128)(2,1)S(1)}, bf16[2,2,512,512]{3,2,1,0:T(8,128)(2,1)S(1)}, bf16...) custom-call(f32[2,4]{1,0:T(2,128)S(1)} %copy-done, ...), custom_call_target="tpu_custom_call" | custom-call | tf_op jit(solution)/shard_map/pallas_call | solution.py:38
  20.5 0.0 collective-permute-done.2.got_ref
  20.5 0.1 shard_map.187.refs_0_.own_ref
  20.6 2.7 %collective-permute-start.3 = (bf16[2,144,128]{2,1,0:T(8,128)(2,1)S(1)}, bf16[2,144,128]{2,1,0:T(8,128)(2,1)S(1)}, u32[]{:S(2)}, u32[]{:S(2)}) collective-permute-start(bf16[2,144,128]{2,1,0:T(8,128)(2,1)S(1)} %shard_map.187.refs_0_.own_ref), channel_id=1, source_target_pairs={{0,8},{1,9},{2,10},{3,11},{4,12},{5,13},{6,14},{7,15},{8,0},{9,1},... | collective-permute-start | bytes 221192 | tf_op jit(solution)/shard_map/ppermute | solution.py:725
  23.4 2.9 %shard_map.188 = (bf16[2,2,512,512]{3,2,1,0:T(8,128)(2,1)S(1)}, bf16[2,2,512,512]{3,2,1,0:T(8,128)(2,1)S(1)}, bf16[1,3,512,512]{3,2,1,0:T(8,128)(2,1)S(1)}, bf16...) custom-call(f32[2,4]{1,0:T(2,128)S(1)} %copy-done, ...), custom_call_target="tpu_custom_call" | custom-call | tf_op jit(solution)/shard_map/pallas_call | solution.py:38
  26.3 0.1 shard_map.189.refs_0_.a_ref
  26.4 1.6 %collective-permute-start.4 = (bf16[2,128,128]{2,1,0:T(8,128)(2,1)S(1)}, bf16[2,128,128]{2,1,0:T(8,128)(2,1)S(1)}, u32[]{:S(2)}, u32[]{:S(2)}) collective-permute-start(bf16[2,128,128]{2,1,0:T(8,128)(2,1)S(1)} %shard_map.189.refs_0_.a_ref), channel_id=1, source_target_pairs={{0,4},{1,5},{2,6},{3,7},{4,0},{5,1},{6,2},{7,3},{8,12},{9,13},{10,... | collective-permute-start | bytes 196616 | tf_op jit(solution)/shard_map/ppermute | solution.py:725
  28.0 3.3 %shard_map.190 = (bf16[2,2,512,512]{3,2,1,0:T(8,128)(2,1)S(1)}, bf16[2,2,512,512]{3,2,1,0:T(8,128)(2,1)S(1)}, bf16[1,3,512,512]{3,2,1,0:T(8,128)(2,1)S(1)}, bf16...) custom-call(f32[2,4]{1,0:T(2,128)S(1)} %copy-done, ...), custom_call_target="tpu_custom_call" | custom-call | tf_op jit(solution)/shard_map/pallas_call | solution.py:38
  31.4 1.6 %collective-permute-start.5 = (bf16[4,128,128]{2,1,0:T(8,128)(2,1)S(1)}, bf16[4,128,128]{2,1,0:T(8,128)(2,1)S(1)}, u32[]{:S(2)}, u32[]{:S(2)}) collective-permute-start(bf16[4,128,128]{2,1,0:T(8,128)(2,1)S(1)} %shard_map.191.refs_0_.a_ref), channel_id=1, source_target_pairs={{0,2},{1,3},{2,0},{3,1},{4,6},{5,7},{6,4},{7,5},{8,10},{9,11},{10,... | collective-permute-start | bytes 393224 | tf_op jit(solution)/shard_map/ppermute | solution.py:725
  33.0 3.8 %shard_map.192 = (bf16[2,2,512,512]{3,2,1,0:T(8,128)(2,1)S(1)}, bf16[2,2,512,512]{3,2,1,0:T(8,128)(2,1)S(1)}, bf16[1,3,512,512]{3,2,1,0:T(8,128)(2,1)S(1)}, bf16...) custom-call(f32[2,4]{1,0:T(2,128)S(1)} %copy-done, ...), custom_call_target="tpu_custom_call" | custom-call | tf_op jit(solution)/shard_map/pallas_call | solution.py:38
  36.8 0.0 collective-permute-done.5.b_ref
  36.8 0.1 collective-permute-start.6
  36.9 1.2 %shard_map.194.rest_4_ = f32[64,512]{1,0:T(8,128)S(1)} custom-call(f32[2,4]{1,0:T(2,128)S(1)} %copy-done, bf16[8,128,128]{2,1,0:T(8,128)(2,1)S(1)} %shard_map.193.rows_ref, bf16[1,3,512,512]{3,2,1,0:T(8,128)(2,1)S(1)} %get-tuple-element.158.rest_0_, bf16[1,3,512,512]{3,2,1,0:T(8,128)(2,1)S(1)} %get-tuple-element.159.rest_1_, ...), custom_call_target="tpu_custom_call" | custom-call | tf_op jit(solution)/shard_map/pallas_call | solution.py:38
  38.1 0.3 collective-permute-done.6.rows_ref
  38.4 1.2 %shard_map.195.refs_0_.own_ref = bf16[64,512]{1,0:T(8,128)(2,1)S(1)} custom-call(f32[2,4]{1,0:T(2,128)S(1)} %copy-done, bf16[8,128,128]{2,1,0:T(8,128)(2,1)S(1)} %collective-permute-done.6.rows_ref, bf16[1,3,512,512]{3,2,1,0:T(8,128)(2,1)S(1)} %get-tuple-element.154.rest_0_, bf16[1,3,512,512]{3,2,1,0:T(8,128)(2,1)S(1)} %get-tuple-element.155.rest_1_, ...), custom_call_target="tpu_custom_call" | custom-call | tf_op jit(solution)/shard_map/pallas_call | solution.py:38
  39.6 1.6 %collective-permute-start.7 = (bf16[64,512]{1,0:T(8,128)(2,1)S(1)}, bf16[64,512]{1,0:T(8,128)(2,1)S(1)}, u32[]{:S(2)}, u32[]{:S(2)}) collective-permute-start(bf16[64,512]{1,0:T(8,128)(2,1)S(1)} %shard_map.195.refs_0_.own_ref), channel_id=1, source_target_pairs={{0,16},{16,0},{1,17},{17,1},{2,18},{18,2},{3,19},{19,3},{4,20},{20... | collective-permute-start | bytes 196616 | tf_op jit(solution)/shard_map/ppermute | solution.py:728
  41.2 2.7 %shard_map.196 = (bf16[2,2,512,512]{3,2,1,0:T(8,128)(2,1)S(1)}, bf16[2,2,512,512]{3,2,1,0:T(8,128)(2,1)S(1)}, bf16[2,2,512,512]{3,2,1,0:T(8,128)(2,1)S(1)}, bf16...) custom-call(f32[2,4]{1,0:T(2,128)S(1)} %copy-done, ...), custom_call_target="tpu_custom_call" | custom-call | tf_op jit(solution)/shard_map/pallas_call | solution.py:38
  43.9 0.1 collective-permute-done.7.got_ref
  44.0 0.2 shard_map.197
  44.2 3.1 %collective-permute-start.8 = (bf16[1,272,128]{2,1,0:T(8,128)(2,1)S(1)}, bf16[1,272,128]{2,1,0:T(8,128)(2,1)S(1)}, u32[]{:S(2)}, u32[]{:S(2)}) collective-permute-start(bf16[1,272,128]{2,1,0:T(8,128)(2,1)S(1)} %get-tuple-element.170.refs_0_.a_ref), channel_id=1, source_target_pairs={{0,8},{1,9},{2,10},{3,11},{4,12},{5,13},{6,14},{7,15},{8,0},{9,1},... | collective-permute-start | bytes 208904 | tf_op jit(solution)/shard_map/ppermute | solution.py:725
  47.3 2.9 %shard_map.198 = (bf16[2,2,512,512]{3,2,1,0:T(8,128)(2,1)S(1)}, bf16[2,2,512,512]{3,2,1,0:T(8,128)(2,1)S(1)}, bf16[1,3,512,512]{3,2,1,0:T(8,128)(2,1)S(1)}, bf16...) custom-call(f32[2,4]{1,0:T(2,128)S(1)} %copy-done, ...), custom_call_target="tpu_custom_call" | custom-call | tf_op jit(solution)/shard_map/pallas_call | solution.py:38
  50.2 0.8 collective-permute-done.8.b_ref
  51.1 1.2 %collective-permute-start.12 = (bf16[2,272,128]{2,1,0:T(8,128)(2,1)S(1)}, bf16[2,272,128]{2,1,0:T(8,128)(2,1)S(1)}, u32[]{:S(2)}, u32[]{:S(2)}) collective-permute-start(bf16[2,272,128]{2,1,0:T(8,128)(2,1)S(1)} %shard_map.199.refs_0_.rest_0_), channel_id=1, source_target_pairs={{0,2},{1,3},{2,0},{3,1},{4,6},{5,7},{6,4},{7,5},{8,10},{9,11},{10,... | collective-permute-start | bytes 417800 | tf_op jit(solution)/shard_map/ppermute | solution.py:725
  52.3 0.2 collective-permute-start.9
  52.5 3.9 %shard_map.200 = (bf16[2,2,512,512]{3,2,1,0:T(8,128)(2,1)S(1)}, bf16[1,2,512,512]{3,2,1,0:T(8,128)(2,1)S(1)}, bf16[1,2,512,512]{3,2,1,0:T(8,128)(2,1)S(1)}, bf16...) custom-call(f32[2,4]{1,0:T(2,128)S(1)} %copy-done, ...), custom_call_target="tpu_custom_call" | custom-call | tf_op jit(solution)/shard_map/pallas_call | solution.py:38
  56.3 0.8 shard_map.201
  57.2 0.0 collective-permute-done.12.b_ref.rest_1_
  57.2 0.2 collective-permute-done.9.a_ref.rest_0_
  57.3 0.1 collective-permute-start.14
  57.4 1.0 %collective-permute-start.10 = (bf16[2,272,128]{2,1,0:T(8,128)(2,1)S(1)}, bf16[2,272,128]{2,1,0:T(8,128)(2,1)S(1)}, u32[]{:S(2)}, u32[]{:S(2)}) collective-permute-start(bf16[2,272,128]{2,1,0:T(8,128)(2,1)S(1)} %collective-permute-done.9.a_ref.rest_0_), channel_id=1, source_target_pairs={{0,2},{1,3},{2,0},{3,1},{4,6},{5,7},{6,4},{7,5},{8,10},{9,11},{10,... | collective-permute-start | bytes 417800 | tf_op jit(solution)/shard_map/ppermute | solution.py:725
  58.4 0.2 collective-permute-start.13
  58.5 5.0 %collective-permute-done.10.rest_0_ = bf16[2,272,128]{2,1,0:T(8,128)(2,1)S(1)} collective-permute-done((bf16[2,272,128]{2,1,0:T(8,128)(2,1)S(1)}, bf16[2,272,128]{2,1,0:T(8,128)(2,1)S(1)}, u32[]{:S(2)}, u32[]{:S(2)}) %collective-permute-start.10) | collective-permute-done | bytes 139296 | tf_op jit(solution)/shard_map/ppermute | solution.py:725
  63.5 3.9 %shard_map.203 = (f32[64,512]{1,0:T(8,128)S(1)}, f32[64,512]{1,0:T(8,128)S(1)}, f32[16,128]{1,0:T(8,128)S(1)}, bf16[1,3,512,512]{3,2,1,0:T(8,128)(2,1)S(1)}, bf1...) custom-call(f32[2,4]{1,0:T(2,128)S(1)} %copy-done, ...), custom_call_target="tpu_custom_call" | custom-call | tf_op jit(solution)/shard_map/pallas_call | solution.py:38
  67.4 0.8 shard_map.204
  68.2 0.0 collective-permute-done.11.rest_0_
  68.2 3.2 %shard_map.205 = (bf16[64,512]{1,0:T(8,128)(2,1)S(1)}, bf16[4,64,512]{2,1,0:T(8,128)(2,1)S(1)}, bf16[4,64,512]{2,1,0:T(8,128)(2,1)S(1)}, bf16[1,3,512,512]{3,2,1...) custom-call(f32[2,4]{1,0:T(2,128)S(1)} %copy-done, ...), custom_call_target="tpu_custom_call" | custom-call | tf_op jit(solution)/shard_map/pallas_call | solution.py:38
  71.4 0.5 collective-permute-start.15
  72.0 0.1 collective-permute-start.16
  72.1 1.2 %shard_map.206.keep_ref = bf16[4,64,512]{2,1,0:T(8,128)(2,1)S(1)} custom-call(f32[2,4]{1,0:T(2,128)S(1)} %copy-done, bf16[64,512]{1,0:T(8,128)(2,1)S(1)} %get-tuple-element.214.x_ref, bf16[4,64,512]{2,1,0:T(8,128)(2,1)S(1)} %get-tuple-element.215.token_ref, bf16[1,3,512,512]{3,2,1,0:T(8,128)(2,1)S(1)} %get-tuple-element.216.rest_0_, ...), custom_call_target="tpu_custom_call" | custom-call | tf_op jit(solution)/shard_map/pallas_call | solution.py:38
  73.3 0.1 shard_map.207
  73.3 1.0 %collective-permute-start.18 = (bf16[2,64,512]{2,1,0:T(8,128)(2,1)S(1)}, bf16[2,64,512]{2,1,0:T(8,128)(2,1)S(1)}, u32[]{:S(2)}, u32[]{:S(2)}) collective-permute-start(bf16[2,64,512]{2,1,0:T(8,128)(2,1)S(1)} %get-tuple-element.221.token_ref), channel_id=1, source_target_pairs={{0,2},{1,3},{2,0},{3,1},{4,6},{5,7},{6,4},{7,5},{8,10},{9,11},{10,... | collective-permute-start | bytes 393224 | tf_op jit(solution)/shard_map/ppermute | solution.py:725
  74.3 1.1 %collective-permute-start.17 = (bf16[2,64,512]{2,1,0:T(8,128)(2,1)S(1)}, bf16[2,64,512]{2,1,0:T(8,128)(2,1)S(1)}, u32[]{:S(2)}, u32[]{:S(2)}) collective-permute-start(bf16[2,64,512]{2,1,0:T(8,128)(2,1)S(1)} %get-tuple-element.227), channel_id=1, source_target_pairs={{0,2},{1,3},{2,0},{3,1},{4,6},{5,7},{6,4},{7,5},{8,10},{9,11},{10,... | collective-permute-start | bytes 393224 | tf_op jit(solution)/shard_map/ppermute | solution.py:725
  75.4 1.2 %shard_map.208.keep_ref = bf16[4,64,512]{2,1,0:T(8,128)(2,1)S(1)} custom-call(f32[2,4]{1,0:T(2,128)S(1)} %copy-done, bf16[64,512]{1,0:T(8,128)(2,1)S(1)} %get-tuple-element.214.x_ref, bf16[2,64,512]{2,1,0:T(8,128)(2,1)S(1)} %get-tuple-element.221.token_ref, bf16[1,3,512,512]{3,2,1,0:T(8,128)(2,1)S(1)} %get-tuple-element.222.rest_0_, ...), custom_call_target="tpu_custom_call" | custom-call | tf_op jit(solution)/shard_map/pallas_call | solution.py:38
  76.6 0.1 shard_map.209
  76.7 3.1 %collective-permute-done.18.got_ref = bf16[2,64,512]{2,1,0:T(8,128)(2,1)S(1)} collective-permute-done((bf16[2,64,512]{2,1,0:T(8,128)(2,1)S(1)}, bf16[2,64,512]{2,1,0:T(8,128)(2,1)S(1)}, u32[]{:S(2)}, u32[]{:S(2)}) %collective-permute-start.18) | collective-permute-done | bytes 131104 | tf_op jit(solution)/shard_map/ppermute | solution.py:725
  79.8 3.0 %collective-permute-start.19 = (bf16[1,64,512]{2,1,0:T(8,128)(2,1)S(1)}, bf16[1,64,512]{2,1,0:T(8,128)(2,1)S(1)}, u32[]{:S(2)}, u32[]{:S(2)}) collective-permute-start(bf16[1,64,512]{2,1,0:T(8,128)(2,1)S(1)} %get-tuple-element.230), channel_id=1, source_target_pairs={{0,12},{1,13},{2,14},{3,15},{4,8},{5,9},{6,10},{7,11},{8,4},{9,5},... | collective-permute-start | bytes 196616 | tf_op jit(solution)/shard_map/ppermute | solution.py:880
  82.9 0.8 collective-permute-start.20
  83.7 1.7 %collective-permute-start.21 = (bf16[1,64,512]{2,1,0:T(8,128)(2,1)S(1)}, bf16[1,64,512]{2,1,0:T(8,128)(2,1)S(1)}, u32[]{:S(2)}, u32[]{:S(2)}) collective-permute-start(bf16[1,64,512]{2,1,0:T(8,128)(2,1)S(1)} %get-tuple-element.232), channel_id=1, source_target_pairs={{0,8},{1,9},{2,10},{3,11},{4,12},{5,13},{6,14},{7,15},{8,0},{9,1},... | collective-permute-start | bytes 196616 | tf_op jit(solution)/shard_map/ppermute | solution.py:880
  85.4 0.7 collective-permute-done.19.refs_1_
  86.0 1.4 %collective-permute-done.20.refs_2_ = bf16[1,64,512]{2,1,0:T(8,128)(2,1)S(1)} collective-permute-done((bf16[1,64,512]{2,1,0:T(8,128)(2,1)S(1)}, bf16[1,64,512]{2,1,0:T(8,128)(2,1)S(1)}, u32[]{:S(2)}, u32[]{:S(2)}) %collective-permute-start.20) | collective-permute-done | bytes 65568 | tf_op jit(solution)/shard_map/ppermute | solution.py:880
  87.5 1.5 %collective-permute-done.21.refs_3_ = bf16[1,64,512]{2,1,0:T(8,128)(2,1)S(1)} collective-permute-done((bf16[1,64,512]{2,1,0:T(8,128)(2,1)S(1)}, bf16[1,64,512]{2,1,0:T(8,128)(2,1)S(1)}, u32[]{:S(2)}, u32[]{:S(2)}) %collective-permute-start.21) | collective-permute-done | bytes 65568 | tf_op jit(solution)/shard_map/ppermute | solution.py:880
  89.0 1.2 %collective-permute-start.22 = (bf16[1,64,512]{2,1,0:T(8,128)(2,1)S(1)}, bf16[1,64,512]{2,1,0:T(8,128)(2,1)S(1)}, u32[]{:S(2)}, u32[]{:S(2)}) collective-permute-start(bf16[1,64,512]{2,1,0:T(8,128)(2,1)S(1)} %shard_map.212.own_ref), channel_id=1, source_target_pairs={{0,16},{16,0},{1,17},{17,1},{2,18},{18,2},{3,19},{19,3},{4,20},{20... | collective-permute-start | bytes 196616 | tf_op jit(solution)/shard_map/ppermute | solution.py:728
  90.2 3.1 %collective-permute-done.22.got_ref = bf16[1,64,512]{2,1,0:T(8,128)(2,1)S(1)} collective-permute-done((bf16[1,64,512]{2,1,0:T(8,128)(2,1)S(1)}, bf16[1,64,512]{2,1,0:T(8,128)(2,1)S(1)}, u32[]{:S(2)}, u32[]{:S(2)}) %collective-permute-start.22) | collective-permute-done | bytes 65568 | tf_op jit(solution)/shard_map/ppermute | solution.py:728
  93.3 0.8 shard_map.213
  (17 shorter events, 0.2 us)
Async XLA Ops:
  0.0 7.2 %copy-start = (f32[2,4]{1,0:T(2,128)S(1)}, f32[2,4]{1,0:T(2,128)}, u32[]{:S(2)}) copy-start(f32[2,4]{1,0:T(2,128)} %scale_ref.33) | copy-start | bytes 100
  6.7 1.8 %collective-permute-start = (bf16[8,144,128]{2,1,0:T(8,128)(2,1)S(1)}, bf16[8,144,128]{2,1,0:T(8,128)(2,1)S(1)}, u32[]{:S(2)}, u32[]{:S(2)}) collective-permute-start(bf16[8,144,128]{2,1,0:T(8,128)(2,1)S(1)} %get-tuple-element.123.refs_0_), channel_id=1, source_target_pairs={{0,1},{1,0},{2,3},{3,2},{4,5},{5,4},{6,7},{7,6},{8,9},{9,8},{10,11... | collective-permute-start | bytes 884744 | tf_op jit(solution)/shard_map/ppermute | solution.py:725
  8.7 7.2 %collective-permute-start.1 = (bf16[4,144,128]{2,1,0:T(8,128)(2,1)S(1)}, bf16[4,144,128]{2,1,0:T(8,128)(2,1)S(1)}, u32[]{:S(2)}, u32[]{:S(2)}) collective-permute-start(bf16[4,144,128]{2,1,0:T(8,128)(2,1)S(1)} %get-tuple-element.128.refs_0_), channel_id=1, source_target_pairs={{0,2},{1,3},{2,0},{3,1},{4,6},{5,7},{6,4},{7,5},{8,10},{9,11},{10,... | collective-permute-start | bytes 442376 | tf_op jit(solution)/shard_map/ppermute | solution.py:725
  16.1 4.4 %collective-permute-start.2 = (bf16[2,144,128]{2,1,0:T(8,128)(2,1)S(1)}, bf16[2,144,128]{2,1,0:T(8,128)(2,1)S(1)}, u32[]{:S(2)}, u32[]{:S(2)}) collective-permute-start(bf16[2,144,128]{2,1,0:T(8,128)(2,1)S(1)} %get-tuple-element.131.refs_0_), channel_id=1, source_target_pairs={{0,4},{1,5},{2,6},{3,7},{4,0},{5,1},{6,2},{7,3},{8,12},{9,13},{10,... | collective-permute-start | bytes 221192 | tf_op jit(solution)/shard_map/ppermute | solution.py:725
  20.6 5.6 %collective-permute-start.3 = (bf16[2,144,128]{2,1,0:T(8,128)(2,1)S(1)}, bf16[2,144,128]{2,1,0:T(8,128)(2,1)S(1)}, u32[]{:S(2)}, u32[]{:S(2)}) collective-permute-start(bf16[2,144,128]{2,1,0:T(8,128)(2,1)S(1)} %shard_map.187.refs_0_.own_ref), channel_id=1, source_target_pairs={{0,8},{1,9},{2,10},{3,11},{4,12},{5,13},{6,14},{7,15},{8,0},{9,1},... | collective-permute-start | bytes 221192 | tf_op jit(solution)/shard_map/ppermute | solution.py:725
  26.4 5.0 %collective-permute-start.4 = (bf16[2,128,128]{2,1,0:T(8,128)(2,1)S(1)}, bf16[2,128,128]{2,1,0:T(8,128)(2,1)S(1)}, u32[]{:S(2)}, u32[]{:S(2)}) collective-permute-start(bf16[2,128,128]{2,1,0:T(8,128)(2,1)S(1)} %shard_map.189.refs_0_.a_ref), channel_id=1, source_target_pairs={{0,4},{1,5},{2,6},{3,7},{4,0},{5,1},{6,2},{7,3},{8,12},{9,13},{10,... | collective-permute-start | bytes 196616 | tf_op jit(solution)/shard_map/ppermute | solution.py:725
  31.4 5.4 %collective-permute-start.5 = (bf16[4,128,128]{2,1,0:T(8,128)(2,1)S(1)}, bf16[4,128,128]{2,1,0:T(8,128)(2,1)S(1)}, u32[]{:S(2)}, u32[]{:S(2)}) collective-permute-start(bf16[4,128,128]{2,1,0:T(8,128)(2,1)S(1)} %shard_map.191.refs_0_.a_ref), channel_id=1, source_target_pairs={{0,2},{1,3},{2,0},{3,1},{4,6},{5,7},{6,4},{7,5},{8,10},{9,11},{10,... | collective-permute-start | bytes 393224 | tf_op jit(solution)/shard_map/ppermute | solution.py:725
  36.8 1.6 %collective-permute-start.6 = (bf16[8,128,128]{2,1,0:T(8,128)(2,1)S(1)}, bf16[8,128,128]{2,1,0:T(8,128)(2,1)S(1)}, u32[]{:S(2)}, u32[]{:S(2)}) collective-permute-start(bf16[8,128,128]{2,1,0:T(8,128)(2,1)S(1)} %shard_map.193.rows_ref), channel_id=1, source_target_pairs={{0,1},{1,0},{2,3},{3,2},{4,5},{5,4},{6,7},{7,6},{8,9},{9,8},{10,11... | collective-permute-start | bytes 786440 | tf_op jit(solution)/shard_map/ppermute | solution.py:725
  39.6 4.3 %collective-permute-start.7 = (bf16[64,512]{1,0:T(8,128)(2,1)S(1)}, bf16[64,512]{1,0:T(8,128)(2,1)S(1)}, u32[]{:S(2)}, u32[]{:S(2)}) collective-permute-start(bf16[64,512]{1,0:T(8,128)(2,1)S(1)} %shard_map.195.refs_0_.own_ref), channel_id=1, source_target_pairs={{0,16},{16,0},{1,17},{17,1},{2,18},{18,2},{3,19},{19,3},{4,20},{20... | collective-permute-start | bytes 196616 | tf_op jit(solution)/shard_map/ppermute | solution.py:728
  44.2 6.8 %collective-permute-start.8 = (bf16[1,272,128]{2,1,0:T(8,128)(2,1)S(1)}, bf16[1,272,128]{2,1,0:T(8,128)(2,1)S(1)}, u32[]{:S(2)}, u32[]{:S(2)}) collective-permute-start(bf16[1,272,128]{2,1,0:T(8,128)(2,1)S(1)} %get-tuple-element.170.refs_0_.a_ref), channel_id=1, source_target_pairs={{0,8},{1,9},{2,10},{3,11},{4,12},{5,13},{6,14},{7,15},{8,0},{9,1},... | collective-permute-start | bytes 208904 | tf_op jit(solution)/shard_map/ppermute | solution.py:725
  51.1 6.1 %collective-permute-start.12 = (bf16[2,272,128]{2,1,0:T(8,128)(2,1)S(1)}, bf16[2,272,128]{2,1,0:T(8,128)(2,1)S(1)}, u32[]{:S(2)}, u32[]{:S(2)}) collective-permute-start(bf16[2,272,128]{2,1,0:T(8,128)(2,1)S(1)} %shard_map.199.refs_0_.rest_0_), channel_id=1, source_target_pairs={{0,2},{1,3},{2,0},{3,1},{4,6},{5,7},{6,4},{7,5},{8,10},{9,11},{10,... | collective-permute-start | bytes 417800 | tf_op jit(solution)/shard_map/ppermute | solution.py:725
  52.3 5.1 %collective-permute-start.9 = (bf16[2,272,128]{2,1,0:T(8,128)(2,1)S(1)}, bf16[2,272,128]{2,1,0:T(8,128)(2,1)S(1)}, u32[]{:S(2)}, u32[]{:S(2)}) collective-permute-start(bf16[2,272,128]{2,1,0:T(8,128)(2,1)S(1)} %shard_map.199.refs_0_.rest_0_), channel_id=1, source_target_pairs={{0,4},{1,5},{2,6},{3,7},{4,0},{5,1},{6,2},{7,3},{8,12},{9,13},{10,... | collective-permute-start | bytes 417800 | tf_op jit(solution)/shard_map/ppermute | solution.py:725
  57.3 6.2 %collective-permute-start.14 = (bf16[4,272,128]{2,1,0:T(8,128)(2,1)S(1)}, bf16[4,272,128]{2,1,0:T(8,128)(2,1)S(1)}, u32[]{:S(2)}, u32[]{:S(2)}) collective-permute-start(bf16[4,272,128]{2,1,0:T(8,128)(2,1)S(1)} %shard_map.202), channel_id=1, source_target_pairs={{0,1},{1,0},{2,3},{3,2},{4,5},{5,4},{6,7},{7,6},{8,9},{9,8},{10,11... | collective-permute-start | bytes 835592 | tf_op jit(solution)/shard_map/ppermute | solution.py:725
  57.4 6.1 %collective-permute-start.10 = (bf16[2,272,128]{2,1,0:T(8,128)(2,1)S(1)}, bf16[2,272,128]{2,1,0:T(8,128)(2,1)S(1)}, u32[]{:S(2)}, u32[]{:S(2)}) collective-permute-start(bf16[2,272,128]{2,1,0:T(8,128)(2,1)S(1)} %collective-permute-done.9.a_ref.rest_0_), channel_id=1, source_target_pairs={{0,2},{1,3},{2,0},{3,1},{4,6},{5,7},{6,4},{7,5},{8,10},{9,11},{10,... | collective-permute-start | bytes 417800 | tf_op jit(solution)/shard_map/ppermute | solution.py:725
  58.4 5.1 %collective-permute-start.13 = (bf16[2,272,128]{2,1,0:T(8,128)(2,1)S(1)}, bf16[2,272,128]{2,1,0:T(8,128)(2,1)S(1)}, u32[]{:S(2)}, u32[]{:S(2)}) collective-permute-start(bf16[2,272,128]{2,1,0:T(8,128)(2,1)S(1)} %shard_map.199.refs_0_.rest_0_), channel_id=1, source_target_pairs={{0,1},{1,0},{2,3},{3,2},{4,5},{5,4},{6,7},{7,6},{8,9},{9,8},{10,11... | collective-permute-start | bytes 417800 | tf_op jit(solution)/shard_map/ppermute | solution.py:725
  63.5 4.7 %collective-permute-start.11 = (bf16[2,272,128]{2,1,0:T(8,128)(2,1)S(1)}, bf16[2,272,128]{2,1,0:T(8,128)(2,1)S(1)}, u32[]{:S(2)}, u32[]{:S(2)}) collective-permute-start(bf16[2,272,128]{2,1,0:T(8,128)(2,1)S(1)} %collective-permute-done.10.rest_0_), channel_id=1, source_target_pairs={{0,1},{1,0},{2,3},{3,2},{4,5},{5,4},{6,7},{7,6},{8,9},{9,8},{10,11... | collective-permute-start | bytes 417800 | tf_op jit(solution)/shard_map/ppermute | solution.py:725
  71.4 1.8 %collective-permute-start.15 = (bf16[4,64,512]{2,1,0:T(8,128)(2,1)S(1)}, bf16[4,64,512]{2,1,0:T(8,128)(2,1)S(1)}, u32[]{:S(2)}, u32[]{:S(2)}) collective-permute-start(bf16[4,64,512]{2,1,0:T(8,128)(2,1)S(1)} %get-tuple-element.220), channel_id=1, source_target_pairs={{0,1},{1,0},{2,3},{3,2},{4,5},{5,4},{6,7},{7,6},{8,9},{9,8},{10,11... | collective-permute-start | bytes 786440 | tf_op jit(solution)/shard_map/ppermute | solution.py:725
  72.0 4.6 %collective-permute-start.16 = (bf16[4,64,512]{2,1,0:T(8,128)(2,1)S(1)}, bf16[4,64,512]{2,1,0:T(8,128)(2,1)S(1)}, u32[]{:S(2)}, u32[]{:S(2)}) collective-permute-start(bf16[4,64,512]{2,1,0:T(8,128)(2,1)S(1)} %get-tuple-element.215.token_ref), channel_id=1, source_target_pairs={{0,1},{1,0},{2,3},{3,2},{4,5},{5,4},{6,7},{7,6},{8,9},{9,8},{10,11... | collective-permute-start | bytes 786440 | tf_op jit(solution)/shard_map/ppermute | solution.py:725
  73.3 6.4 %collective-permute-start.18 = (bf16[2,64,512]{2,1,0:T(8,128)(2,1)S(1)}, bf16[2,64,512]{2,1,0:T(8,128)(2,1)S(1)}, u32[]{:S(2)}, u32[]{:S(2)}) collective-permute-start(bf16[2,64,512]{2,1,0:T(8,128)(2,1)S(1)} %get-tuple-element.221.token_ref), channel_id=1, source_target_pairs={{0,2},{1,3},{2,0},{3,1},{4,6},{5,7},{6,4},{7,5},{8,10},{9,11},{10,... | collective-permute-start | bytes 393224 | tf_op jit(solution)/shard_map/ppermute | solution.py:725
  74.3 9.4 %collective-permute-start.17 = (bf16[2,64,512]{2,1,0:T(8,128)(2,1)S(1)}, bf16[2,64,512]{2,1,0:T(8,128)(2,1)S(1)}, u32[]{:S(2)}, u32[]{:S(2)}) collective-permute-start(bf16[2,64,512]{2,1,0:T(8,128)(2,1)S(1)} %get-tuple-element.227), channel_id=1, source_target_pairs={{0,2},{1,3},{2,0},{3,1},{4,6},{5,7},{6,4},{7,5},{8,10},{9,11},{10,... | collective-permute-start | bytes 393224 | tf_op jit(solution)/shard_map/ppermute | solution.py:725
  79.8 6.2 %collective-permute-start.19 = (bf16[1,64,512]{2,1,0:T(8,128)(2,1)S(1)}, bf16[1,64,512]{2,1,0:T(8,128)(2,1)S(1)}, u32[]{:S(2)}, u32[]{:S(2)}) collective-permute-start(bf16[1,64,512]{2,1,0:T(8,128)(2,1)S(1)} %get-tuple-element.230), channel_id=1, source_target_pairs={{0,12},{1,13},{2,14},{3,15},{4,8},{5,9},{6,10},{7,11},{8,4},{9,5},... | collective-permute-start | bytes 196616 | tf_op jit(solution)/shard_map/ppermute | solution.py:880
  82.9 4.6 %collective-permute-start.20 = (bf16[1,64,512]{2,1,0:T(8,128)(2,1)S(1)}, bf16[1,64,512]{2,1,0:T(8,128)(2,1)S(1)}, u32[]{:S(2)}, u32[]{:S(2)}) collective-permute-start(bf16[1,64,512]{2,1,0:T(8,128)(2,1)S(1)} %get-tuple-element.231), channel_id=1, source_target_pairs={{0,4},{1,5},{2,6},{3,7},{4,0},{5,1},{6,2},{7,3},{8,12},{9,13},{10,... | collective-permute-start | bytes 196616 | tf_op jit(solution)/shard_map/ppermute | solution.py:880
  83.7 5.2 %collective-permute-start.21 = (bf16[1,64,512]{2,1,0:T(8,128)(2,1)S(1)}, bf16[1,64,512]{2,1,0:T(8,128)(2,1)S(1)}, u32[]{:S(2)}, u32[]{:S(2)}) collective-permute-start(bf16[1,64,512]{2,1,0:T(8,128)(2,1)S(1)} %get-tuple-element.232), channel_id=1, source_target_pairs={{0,8},{1,9},{2,10},{3,11},{4,12},{5,13},{6,14},{7,15},{8,0},{9,1},... | collective-permute-start | bytes 196616 | tf_op jit(solution)/shard_map/ppermute | solution.py:880
  89.0 4.3 %collective-permute-start.22 = (bf16[1,64,512]{2,1,0:T(8,128)(2,1)S(1)}, bf16[1,64,512]{2,1,0:T(8,128)(2,1)S(1)}, u32[]{:S(2)}, u32[]{:S(2)}) collective-permute-start(bf16[1,64,512]{2,1,0:T(8,128)(2,1)S(1)} %shard_map.212.own_ref), channel_id=1, source_target_pairs={{0,16},{16,0},{1,17},{17,1},{2,18},{18,2},{3,19},{19,3},{4,20},{20... | collective-permute-start | bytes 196616 | tf_op jit(solution)/shard_map/ppermute | solution.py:728
